TPU v7x, 256 devices: a whole 4x4x8 slice. The times are simulated.
256 devices in a mesh: req: 32 (over z, y_lo, core), ctx: 8 (over x, y_hi).
Axes of the slice: x: 4, y: 4 (y_hi: 2, y_lo: 2; y = y_hi * 2 + y_lo), z: 8, core: 2. Of those that a mesh axis runs over, the one named last changes fastest.
Arguments:
- queries: bfloat16 [32, 128, 4096], P('req', 'ctx'), may hold values from -6 to 6
- fresh_kv: bfloat16 [32, 128, 1024], P('req', 'ctx'), may hold values from -6 to 6
- cache_pages: bfloat16 [32, 8, 32, 64, 1024], P('req', 'ctx'), may hold values from -400 to 400
- stretch_store: int32 [32, 8, 32], P('req', 'ctx'), may hold values from 0 to 31, as said below
- stretch_request: int32 [32, 8, 32], P('req', 'ctx'), may hold values from 0 to 31, as said below
- recompute_idx: int32 [32, 8, 16], P('req'), may hold values from 0 to 2047, as said below
- block_mask: int32 [32, 8, 2, 8, 32], P('req'), may hold values 0 or 1
Outputs:
- attended: bfloat16 [32, 128, 4096], P('req', 'ctx')
- joined_cache: bfloat16 [32, 16384, 1024], P('req', 'ctx')
Inputs may be any that keep to these rules, and one draw needn't show every extreme that they name: The page at position j of request r's shard on ctx index c lies on store stretch_store[r, c, j] of the same ctx index; the 32 pages of one shard lie on 32 different stores. `stretch_request`: A store's 32 slots belong to 32 different requests, and for each entry of stretch_store exactly one slot of the named store names that request. `recompute_idx`: within a shard the indices are distinct and increasing and include 0 and 2047.
All inputs are finite; a program needn't handle non-finite values. No bound on the sum of `block_mask` on one device may be relied on, other than what follows from the above.
Results may differ from a plain program's by a relative error of at most 0.02.
The roundings to bfloat16 on the way count: a program that leaves them out, or rounds other values in their place, can miss the bound.
Values may be sent and summed in bfloat16 or wider, within the bound.
No kernel may reach another device: no remote copies, remote signals or barrier semaphores. Data moves between devices by JAX's collectives and lax.ppermute only.
A program may use at most 64 MiB of HBM per device.

v0:
```python
import math

import jax
import jax.numpy as jnp
from jax import lax
from jax.sharding import PartitionSpec as P

QHEADS = 32
KVHEADS = 4
HEAD = 128
TILE = 8


THETA = 500000.0
NEG = -1e30


def passed_along(value, axis, steps):
    count = lax.axis_size(axis)
    pairs = [(source, (source + steps) % count) for source in range(count)]
    return lax.ppermute(value, axis, pairs)


def rotary(values, position, head_count):
    number = values.shape[0]
    half_size = HEAD // 2
    frequency = jnp.exp(-(2.0 * jnp.arange(half_size, dtype=jnp.float32) / HEAD) * math.log(THETA))
    angles = position.astype(jnp.float32)[:, None] * frequency[None, :]
    cosine = jnp.cos(angles)[:, None, :]
    sine = jnp.sin(angles)[:, None, :]
    shaped = values.astype(jnp.float32).reshape(number, head_count, HEAD)
    first_half = shaped[..., :half_size]
    second_half = shaped[..., half_size:]
    turned = jnp.concatenate(
        [first_half * cosine - second_half * sine, second_half * cosine + first_half * sine],
        axis=-1,
    )
    return turned.reshape(number, head_count * HEAD)


def local(
    queries, fresh_kv, cache_pages, stretch_store, stretch_request, recompute_idx, block_mask
):
    shard_count = lax.axis_size("ctx")
    device = lax.axis_index("ctx")
    store_count = lax.axis_size("req")
    feature = KVHEADS * HEAD
    groups = QHEADS // KVHEADS
    page_len = cache_pages.shape[3]
    page_count = cache_pages.shape[2]
    span_len = page_count * page_len
    row_count = queries.shape[1]
    query_width = queries.shape[2]
    tile_count = row_count // TILE
    targets = stretch_request[0, 0]
    selector = (jnp.arange(store_count, dtype=jnp.int32)[:, None] == targets[None, :]).astype(
        jnp.bfloat16
    )
    outgoing = jnp.einsum(
        "dt,tuf->duf", selector, cache_pages[0, 0], preferred_element_type=jnp.float32
    ).astype(jnp.bfloat16)
    local_idx = recompute_idx[0]
    own_idx = lax.dynamic_index_in_dim(local_idx, device, 0, keepdims=False)
    own_pos = device * span_len + own_idx
    fresh_rows = fresh_kv[0]
    turned = rotary(fresh_rows[:, :feature], own_pos, KVHEADS)
    new_rows = jnp.concatenate(
        [turned, fresh_rows[:, feature:].astype(jnp.float32)], axis=1
    ).astype(jnp.bfloat16)
    rotated = rotary(queries[0], own_pos, QHEADS).astype(jnp.bfloat16)
    incoming = lax.all_to_all(outgoing, "req", split_axis=0, concat_axis=0, tiled=True)
    assembled = jnp.take(incoming, stretch_store[0, 0], axis=0).reshape(span_len, 2 * feature)
    joined_rows = assembled.at[own_idx].set(new_rows)
    key_rows = joined_rows[:, :feature].reshape(span_len, KVHEADS, HEAD)
    value_rows = joined_rows[:, feature:].reshape(span_len, KVHEADS, HEAD)
    mask_cols = lax.dynamic_index_in_dim(block_mask[0], device, 2, keepdims=False)
    key_pos = device * span_len + jnp.arange(span_len, dtype=jnp.int32)

    def allowed_for(source):
        position = source * span_len + lax.dynamic_index_in_dim(
            local_idx, source, 0, keepdims=False
        )
        tile_mask = lax.dynamic_index_in_dim(mask_cols, source, 0, keepdims=False) == 1
        per_key = jnp.broadcast_to(
            tile_mask[:, None, :, None], (tile_count, TILE, page_count, page_len)
        ).reshape(row_count, span_len)
        causal = key_pos[None, :] <= position[:, None]
        same_page = (key_pos // page_len)[None, :] == (position // page_len)[:, None]
        return causal & (same_page | per_key)

    def attend(query_part, key_part, value_part, allowed):
        kv_count = key_part.shape[1]
        heads_here = kv_count * groups
        query_rows = query_part.reshape(row_count, kv_count, groups, HEAD)
        scores = jnp.einsum(
            "rkgd,skd->kgrs", query_rows, key_part, preferred_element_type=jnp.float32
        ) / math.sqrt(HEAD)
        masked = jnp.where(allowed, scores, NEG)
        block_max = jnp.max(masked, axis=-1)
        weights = jnp.where(allowed, jnp.exp(masked - block_max[..., None]), 0.0)
        block_total = jnp.sum(weights, axis=-1)
        rounded = weights.astype(jnp.bfloat16)
        mixture = jnp.einsum(
            "kgrs,skd->rkgd", rounded, value_part, preferred_element_type=jnp.float32
        )
        return (
            mixture.reshape(row_count, heads_here * HEAD),
            jnp.transpose(block_max, (2, 0, 1)).reshape(row_count, heads_here),
            jnp.transpose(block_total, (2, 0, 1)).reshape(row_count, heads_here),
        )

    def block_part(query_part, key_part, value_part, source):
        allowed = allowed_for(source)
        return attend(query_part, key_part, value_part, allowed)

    def place(records, result, source, head_start):
        out_parts, max_parts, sum_parts = records
        mixture, block_max, block_total = result
        zero_index = jnp.int32(0)
        out_parts = lax.dynamic_update_slice(
            out_parts, mixture[None], (source, zero_index, jnp.int32(head_start * HEAD))
        )
        max_parts = lax.dynamic_update_slice(
            max_parts, block_max[None], (source, zero_index, jnp.int32(head_start))
        )
        sum_parts = lax.dynamic_update_slice(
            sum_parts, block_total[None], (source, zero_index, jnp.int32(head_start))
        )
        return (out_parts, max_parts, sum_parts)

    initial = (
        jnp.zeros((shard_count, row_count, query_width), jnp.float32),
        jnp.full((shard_count, row_count, QHEADS), NEG, jnp.float32),
        jnp.zeros((shard_count, row_count, QHEADS), jnp.float32),
    )

    def visit_one(step_index, visiting, records):
        source = (device - step_index) % shard_count
        return place(records, block_part(visiting, key_rows, value_rows, source), source, 0)

    def turn_one(step_index, carry):
        visiting, records = carry
        records = visit_one(step_index, visiting, records)
        visiting = passed_along(visiting, "ctx", 1)
        return (visiting, records)

    visiting, records = lax.fori_loop(0, shard_count - 1, turn_one, (rotated, initial))
    records = visit_one(shard_count - 1, visiting, records)
    out_parts, max_parts, sum_parts = records
    out_all = lax.all_to_all(out_parts, "ctx", split_axis=0, concat_axis=0, tiled=True)
    max_all = lax.all_to_all(max_parts, "ctx", split_axis=0, concat_axis=0, tiled=True)
    sum_all = lax.all_to_all(sum_parts, "ctx", split_axis=0, concat_axis=0, tiled=True)
    source_count = out_all.shape[0]
    here_rows = out_all.shape[1]
    top_max = jnp.max(max_all, axis=0)
    factor = jnp.exp(max_all - top_max[None])
    row_total = jnp.sum(sum_all * factor, axis=0)
    shaped = out_all.reshape(source_count, here_rows, QHEADS, HEAD)
    merged = jnp.sum(shaped * factor[..., None], axis=0) / row_total[..., None]
    attended = merged.reshape(here_rows, QHEADS * HEAD).astype(jnp.bfloat16)
    return (attended[None], joined_rows[None])


def solution(mesh):
    return jax.shard_map(
        local,
        mesh=mesh,
        in_specs=(
            P("req", "ctx", None),
            P("req", "ctx", None),
            P("req", "ctx", None, None, None),
            P("req", "ctx", None),
            P("req", "ctx", None),
            P("req", None, None),
            P("req", None, None, None, None),
        ),
        out_specs=(P("req", "ctx", None), P("req", "ctx", None)),
        check_vma=False,
    )
```

profile of v0, /device:TPU:32, one launch (start us, length us, event | category | flops | bytes accessed | tf_op | source)
XLA Modules:
  0.0 308.0 jit_solution(1465773212597862540)
XLA Ops:
  0.6 7.9 %fusion.37 = bf16[32,64,1024]{2,0,1:T(8,128)(2,1)S(1)} fusion(bf16[32,64,1024]{2,1,0:T(8,128)(2,1)} %bitcast.167, s32[32]{0:T(128)} %bitcast.182), kind=kOutput, calls=%fused_computation.54 | convolution fusion | flops 136315904 | bytes 8388736 | tf_op jit(solution)/shard_map/dt,tuf->duf/dot_general | solution.py:59
  8.6 4.3 %copy.30 = bf16[32,64,1024]{2,1,0:T(8,128)(2,1)} copy(bf16[32,64,1024]{2,0,1:T(8,128)(2,1)S(1)} %fusion.37) | data formatting | bytes 8388608 | tf_op jit(solution)/shard_map/convert_element_type | solution.py:61
  12.9 9.9 %all-to-all-start = ((bf16[32,64,1024]{2,1,0:T(8,128)(2,1)}), bf16[32,64,1024]{2,1,0:T(8,128)(2,1)}, u32[]{:S(2)}, u32[]{:S(2)}) async-start(bf16[32,64,1024]{2,1,0:T(8,128)(2,1)} %copy.30), calls=%async_computation | async-start | bytes 8388608 | tf_op jit(solution)/shard_map/all_to_all | solution.py:71
  25.9 92.4 %all-to-all-done = bf16[32,64,1024]{2,1,0:T(8,128)(2,1)} async-done(((bf16[32,64,1024]{2,1,0:T(8,128)(2,1)}), bf16[32,64,1024]{2,1,0:T(8,128)(2,1)}, u32[]{:S(2)}, u32[]{:S(2)}) %all-to-all-start) | async-done | bytes 4194336 | tf_op jit(solution)/shard_map/all_to_all | solution.py:71
  118.4 5.0 %gather_fusion = bf16[32,64,1024]{2,1,0:T(8,128)(2,1)} fusion(bf16[32,64,1024]{2,1,0:T(8,128)(2,1)} %all-to-all-done, s32[1024]{0:T(1024)S(1)} %pad_clamp_fusion), kind=kCustom, calls=%fused_computation | custom fusion | bytes 8388736 | tf_op jit(solution)/shard_map/jit(_take)/gather | solution.py:72
  123.3 3.9 %bitcast_select_fusion.2 = bf16[2048,1024]{1,0:T(8,128)(2,1)} fusion(bf16[32,64,1024]{2,1,0:T(8,128)(2,1)} %gather_fusion, pred[2048]{0:T(1024)(128)(4,1)S(1)} %broadcast_in_dim.139), kind=kLoop, calls=%fused_computation.47 | loop fusion | flops 2097152 | bytes 8390656 | tf_op jit(solution)/shard_map/jit(_take)/select_n | solution.py:72
  127.2 5.8 %scatter_custom_fusion = bf16[2048,1024]{1,0:T(8,128)(2,1)} fusion(bf16[2048,1024]{1,0:T(8,128)(2,1)} %bitcast_select_fusion.2, s32[16]{0:T(128)S(1)} %fusion.63, bf16[16,512]{1,0:T(8,128)(2,1)S(1)} %get-tuple-element.449, bf16[]{:T(256)} %constant.292, bf16[16,512]{1,0:T(8,128)(2,1)S(1)} %bitcast.175), kind=kCustom, calls=%fused_computation.71 | custom fusion | flops 65536 | bytes 4227584 | tf_op jit(solution)/shard_map/scatter | solution.py:73
  133.0 4.4 %fusion.69 = (bf16[2048,512]{1,0:T(8,128)(2,1)}, bf16[2048,512]{1,0:T(8,128)(2,1)}) fusion(bf16[2048,1024]{1,0:T(8,128)(2,1)} %scatter_custom_fusion), kind=kLoop, calls=%fused_computation.121 | loop fusion | bytes 8388608 | tf_op jit(solution)/shard_map/slice | solution.py:75
  137.4 2.9 copy.31
  140.3 2.6 copy.33
  143.0 2.9 copy.32
  145.9 2.5 copy.34
  149.9 94.9 %while.24 = (s32[]{:T(128)}, bf16[16,4096]{1,0:T(8,128)(2,1)S(1)}, f32[8,16,4096]{2,1,0:T(8,128)}, f32[8,16,32]{2,1,0:T(8,128)S(1)}, f32[8,16,32]{2,1,0:T(8,128)...) while((s32[]{:T(128)}, bf16[16,4096]{1,0:T(8,128)(2,1)S(1)}, ...), condition=%wide.region_4.5_spmd.clone.clone, body=%wide.region_1.4_spmd.clone.clone.sunk | while | flops 550669696 | bytes 36934756 | solution.py:147
  150.0 3.0 collective-permute-start
  153.5 2.5 fusion.81
  156.0 1.9 copy-done
  159.2 4.0 %fusion.82 = f32[16,4,8,128]{3,0,2,1:T(8,128)S(1)} fusion(bf16[2048,4,128]{2,0,1:T(8,128)(2,1)} %get-tuple-element.576, f32[4,2048,16,8]{1,2,3,0:T(8,128)} %copy-done, f32[4,8,16]{2,1,0:T(8,128)S(1)} %get-tuple-element.534, pred[16,2048]{1,0:T(8,128)(4,1)S(1)} %or_and_fusion.3), kind=kOutput, calls=%fused_computation.18.clone.1 | convolution fusion | flops 273678336 | bytes 6588416 | tf_op jit(solution)/shard_map/while/body/eval_jaxpr/kgrs,skd->rkgd/dot_general | solution.py:103
  166.3 2.5 fusion.81
  168.8 1.9 copy-done
  172.0 4.0 %fusion.82 = f32[16,4,8,128]{3,0,2,1:T(8,128)S(1)} fusion(bf16[2048,4,128]{2,0,1:T(8,128)(2,1)} %get-tuple-element.576, f32[4,2048,16,8]{1,2,3,0:T(8,128)} %copy-done, f32[4,8,16]{2,1,0:T(8,128)S(1)} %get-tuple-element.534, pred[16,2048]{1,0:T(8,128)(4,1)S(1)} %or_and_fusion.3), kind=kOutput, calls=%fused_computation.18.clone.1 | convolution fusion | flops 273678336 | bytes 6588416 | tf_op jit(solution)/shard_map/while/body/eval_jaxpr/kgrs,skd->rkgd/dot_general | solution.py:103
  177.0 3.0 collective-permute-start
  180.5 2.5 fusion.81
  183.0 1.9 copy-done
  186.2 4.0 %fusion.82 = f32[16,4,8,128]{3,0,2,1:T(8,128)S(1)} fusion(bf16[2048,4,128]{2,0,1:T(8,128)(2,1)} %get-tuple-element.576, f32[4,2048,16,8]{1,2,3,0:T(8,128)} %copy-done, f32[4,8,16]{2,1,0:T(8,128)S(1)} %get-tuple-element.534, pred[16,2048]{1,0:T(8,128)(4,1)S(1)} %or_and_fusion.3), kind=kOutput, calls=%fused_computation.18.clone.1 | convolution fusion | flops 273678336 | bytes 6588416 | tf_op jit(solution)/shard_map/while/body/eval_jaxpr/kgrs,skd->rkgd/dot_general | solution.py:103
  193.3 2.5 fusion.81
  195.8 1.9 copy-done
  199.0 4.0 %fusion.82 = f32[16,4,8,128]{3,0,2,1:T(8,128)S(1)} fusion(bf16[2048,4,128]{2,0,1:T(8,128)(2,1)} %get-tuple-element.576, f32[4,2048,16,8]{1,2,3,0:T(8,128)} %copy-done, f32[4,8,16]{2,1,0:T(8,128)S(1)} %get-tuple-element.534, pred[16,2048]{1,0:T(8,128)(4,1)S(1)} %or_and_fusion.3), kind=kOutput, calls=%fused_computation.18.clone.1 | convolution fusion | flops 273678336 | bytes 6588416 | tf_op jit(solution)/shard_map/while/body/eval_jaxpr/kgrs,skd->rkgd/dot_general | solution.py:103
  204.0 3.0 collective-permute-start
  207.5 2.5 fusion.81
  210.0 1.9 copy-done
  213.2 4.0 %fusion.82 = f32[16,4,8,128]{3,0,2,1:T(8,128)S(1)} fusion(bf16[2048,4,128]{2,0,1:T(8,128)(2,1)} %get-tuple-element.576, f32[4,2048,16,8]{1,2,3,0:T(8,128)} %copy-done, f32[4,8,16]{2,1,0:T(8,128)S(1)} %get-tuple-element.534, pred[16,2048]{1,0:T(8,128)(4,1)S(1)} %or_and_fusion.3), kind=kOutput, calls=%fused_computation.18.clone.1 | convolution fusion | flops 273678336 | bytes 6588416 | tf_op jit(solution)/shard_map/while/body/eval_jaxpr/kgrs,skd->rkgd/dot_general | solution.py:103
  220.0 2.5 fusion.81
  222.6 1.9 copy-done
  225.7 4.0 %fusion.82 = f32[16,4,8,128]{3,0,2,1:T(8,128)S(1)} fusion(bf16[2048,4,128]{2,0,1:T(8,128)(2,1)} %get-tuple-element.576, f32[4,2048,16,8]{1,2,3,0:T(8,128)} %copy-done, f32[4,8,16]{2,1,0:T(8,128)S(1)} %get-tuple-element.534, pred[16,2048]{1,0:T(8,128)(4,1)S(1)} %or_and_fusion.3), kind=kOutput, calls=%fused_computation.18.clone.1 | convolution fusion | flops 273678336 | bytes 6588416 | tf_op jit(solution)/shard_map/while/body/eval_jaxpr/kgrs,skd->rkgd/dot_general | solution.py:103
  230.7 3.0 collective-permute-start
  234.2 2.5 fusion.81
  236.7 1.9 copy-done
  239.9 4.0 %fusion.82 = f32[16,4,8,128]{3,0,2,1:T(8,128)S(1)} fusion(bf16[2048,4,128]{2,0,1:T(8,128)(2,1)} %get-tuple-element.576, f32[4,2048,16,8]{1,2,3,0:T(8,128)} %copy-done, f32[4,8,16]{2,1,0:T(8,128)S(1)} %get-tuple-element.534, pred[16,2048]{1,0:T(8,128)(4,1)S(1)} %or_and_fusion.3), kind=kOutput, calls=%fused_computation.18.clone.1 | convolution fusion | flops 273678336 | bytes 6588416 | tf_op jit(solution)/shard_map/while/body/eval_jaxpr/kgrs,skd->rkgd/dot_general | solution.py:103
  244.9 4.4 %fusion.34 = (f32[4,8,16]{2,1,0:T(8,128)S(1)}, f32[4,2048,16,8]{1,2,3,0:T(8,128)}) fusion(pred[16,2048]{1,0:T(8,128)(4,1)S(1)} %or_and_fusion.1, bf16[2048,4,128,1]{0,2,3,1:T(8,128)(2,1)} %bitcast.164, bf16[16,4,8,128]{3,2,1,0:T(8,128)(2,1)S(1)} %bitcast.174), kind=kOutput, calls=%fused_computation.51 | convolution fusion | flops 271580672 | bytes 6457344 | tf_op jit(solution)/shard_map/rkgd,skd->kgrs/dot_general | solution.py:95
  250.1 4.3 %all-to-all-start.2 = ((f32[8,1,512]{2,1,0:T(1,128)}), f32[8,1,512]{2,1,0:T(1,128)S(1)}, u32[]{:S(2)}, u32[]{:S(2)}) async-start(f32[8,1,512]{2,1,0:T(1,128)} %reshape.451), calls=%async_computation.2 | async-start | bytes 32768 | tf_op jit(solution)/shard_map/all_to_all | solution.py:151
  254.3 3.4 %fusion.35 = f32[4,8,16]{2,1,0:T(8,128)S(1)} fusion(f32[4,2048,16,8]{1,2,3,0:T(8,128)} %get-tuple-element.453, f32[4,8,16]{2,1,0:T(8,128)S(1)} %get-tuple-element.452, pred[16,2048]{1,0:T(8,128)(4,1)S(1)} %or_and_fusion.1), kind=kLoop, calls=%fused_computation.52 | loop fusion | flops 5242368 | bytes 4231168 | tf_op jit(solution)/shard_map/reduce_sum | solution.py:101
  257.8 3.3 %fusion.43 = f32[16,4,8,128]{3,0,2,1:T(8,128)S(1)} fusion(bf16[2048,4,128,1]{0,2,3,1:T(8,128)(2,1)S(1)} %bitcast.162, f32[4,2048,16,8]{1,2,3,0:T(8,128)} %get-tuple-element.453, f32[4,8,16]{2,1,0:T(8,128)S(1)} %get-tuple-element.452, pred[16,2048]{1,0:T(8,128)(4,1)S(1)} %or_and_fusion.1), kind=kOutput, calls=%fused_computation.58 | convolution fusion | flops 273678336 | bytes 6588416 | tf_op jit(solution)/shard_map/kgrs,skd->rkgd/dot_general | solution.py:103
  262.0 7.1 %all-to-all-start.3 = ((f32[8,1,512]{2,1,0:T(1,128)}), f32[8,1,512]{2,1,0:T(1,128)S(1)}, u32[]{:S(2)}, u32[]{:S(2)}) async-start(f32[8,1,512]{2,1,0:T(1,128)} %reshape.449), calls=%async_computation.3 | async-start | bytes 32768 | tf_op jit(solution)/shard_map/all_to_all | solution.py:152
  269.9 7.0 %all-to-all-done.3 = f32[8,1,512]{2,1,0:T(1,128)S(1)} async-done(((f32[8,1,512]{2,1,0:T(1,128)}), f32[8,1,512]{2,1,0:T(1,128)S(1)}, u32[]{:S(2)}, u32[]{:S(2)}) %all-to-all-start.3) | async-done | bytes 16416 | tf_op jit(solution)/shard_map/all_to_all | solution.py:152
  276.8 3.6 %all-to-all-start.1 = ((f32[8,16,4096]{2,1,0:T(8,128)}), f32[8,16,4096]{2,1,0:T(8,128)S(1)}, u32[]{:S(2)}, u32[]{:S(2)}) async-start(f32[8,16,4096]{2,1,0:T(8,128)} %constant_dynamic-update-slice_fusion.5), calls=%async_computation.1 | async-start | bytes 4194304 | tf_op jit(solution)/shard_map/all_to_all | solution.py:150
  282.5 1.9 mul.144
  284.4 2.8 mul.145
  287.4 18.1 %all-to-all-done.1 = f32[8,16,4096]{2,1,0:T(8,128)S(1)} async-done(((f32[8,16,4096]{2,1,0:T(8,128)}), f32[8,16,4096]{2,1,0:T(8,128)S(1)}, u32[]{:S(2)}, u32[]{:S(2)}) %all-to-all-start.1) | async-done | bytes 2097184 | tf_op jit(solution)/shard_map/all_to_all | solution.py:150
  (205 shorter events, 35.1 us)
Async XLA Ops:
  12.9 10.0 %copy-start.3 = (bf16[1,16,1024]{2,1,0:T(8,128)(2,1)S(1)}, bf16[1,16,1024]{2,1,0:T(8,128)(2,1)}, u32[]{:S(2)}) copy-start(bf16[1,16,1024]{2,1,0:T(8,128)(2,1)} %param.10) | copy-start | bytes 98308
  12.9 10.1 %copy-start.4 = (s32[1,8,16]{2,1,0:T(8,128)S(1)}, s32[1,8,16]{2,1,0:T(8,128)}, u32[]{:S(2)}) copy-start(s32[1,8,16]{2,1,0:T(8,128)} %param.14) | copy-start | bytes 1540
  12.9 10.4 %copy-start.5 = (s32[1,1,32]{2,1,0:T(1,128)S(1)}, s32[1,1,32]{2,1,0:T(1,128)}, u32[]{:S(2)}) copy-start(s32[1,1,32]{2,1,0:T(1,128)} %param.12) | copy-start | bytes 388
  12.9 10.6 %copy-start.2 = (bf16[1,16,4096]{2,1,0:T(8,128)(2,1)S(1)}, bf16[1,16,4096]{2,1,0:T(8,128)(2,1)}, u32[]{:S(2)}) copy-start(bf16[1,16,4096]{2,1,0:T(8,128)(2,1)} %param.9) | copy-start | bytes 393220
  12.9 105.5 %all-to-all-start = ((bf16[32,64,1024]{2,1,0:T(8,128)(2,1)}), bf16[32,64,1024]{2,1,0:T(8,128)(2,1)}, u32[]{:S(2)}, u32[]{:S(2)}) async-start(bf16[32,64,1024]{2,1,0:T(8,128)(2,1)} %copy.30), calls=%async_computation | async-start | bytes 8388608 | tf_op jit(solution)/shard_map/all_to_all | solution.py:71
  140.3 2.6 copy-start.1
  150.0 14.2 %collective-permute-start = (bf16[16,4096]{1,0:T(8,128)(2,1)S(1)}, bf16[16,4096]{1,0:T(8,128)(2,1)S(1)}, u32[]{:S(2)}, u32[]{:S(2)}) collective-permute-start(bf16[16,4096]{1,0:T(8,128)(2,1)S(1)} %copy.105), channel_id=1, source_target_pairs={{0,1},{1,2},{2,3},{3,4},{4,5},{5,6},{6,7},{7,0},{8,9},{9,10},{10,1... | collective-permute-start | bytes 393224 | tf_op jit(solution)/shard_map/while/body/eval_jaxpr/ppermute | solution.py:21
  156.0 1.9 copy-start
  164.2 12.8 %collective-permute-start = (bf16[16,4096]{1,0:T(8,128)(2,1)S(1)}, bf16[16,4096]{1,0:T(8,128)(2,1)S(1)}, u32[]{:S(2)}, u32[]{:S(2)}) collective-permute-start(bf16[16,4096]{1,0:T(8,128)(2,1)S(1)} %copy.105), channel_id=1, source_target_pairs={{0,1},{1,2},{2,3},{3,4},{4,5},{5,6},{6,7},{7,0},{8,9},{9,10},{10,1... | collective-permute-start | bytes 393224 | tf_op jit(solution)/shard_map/while/body/eval_jaxpr/ppermute | solution.py:21
  168.8 1.9 copy-start
  177.0 14.2 %collective-permute-start = (bf16[16,4096]{1,0:T(8,128)(2,1)S(1)}, bf16[16,4096]{1,0:T(8,128)(2,1)S(1)}, u32[]{:S(2)}, u32[]{:S(2)}) collective-permute-start(bf16[16,4096]{1,0:T(8,128)(2,1)S(1)} %copy.105), channel_id=1, source_target_pairs={{0,1},{1,2},{2,3},{3,4},{4,5},{5,6},{6,7},{7,0},{8,9},{9,10},{10,1... | collective-permute-start | bytes 393224 | tf_op jit(solution)/shard_map/while/body/eval_jaxpr/ppermute | solution.py:21
  183.0 1.9 copy-start
  191.2 12.8 %collective-permute-start = (bf16[16,4096]{1,0:T(8,128)(2,1)S(1)}, bf16[16,4096]{1,0:T(8,128)(2,1)S(1)}, u32[]{:S(2)}, u32[]{:S(2)}) collective-permute-start(bf16[16,4096]{1,0:T(8,128)(2,1)S(1)} %copy.105), channel_id=1, source_target_pairs={{0,1},{1,2},{2,3},{3,4},{4,5},{5,6},{6,7},{7,0},{8,9},{9,10},{10,1... | collective-permute-start | bytes 393224 | tf_op jit(solution)/shard_map/while/body/eval_jaxpr/ppermute | solution.py:21
  195.8 1.9 copy-start
  204.0 14.2 %collective-permute-start = (bf16[16,4096]{1,0:T(8,128)(2,1)S(1)}, bf16[16,4096]{1,0:T(8,128)(2,1)S(1)}, u32[]{:S(2)}, u32[]{:S(2)}) collective-permute-start(bf16[16,4096]{1,0:T(8,128)(2,1)S(1)} %copy.105), channel_id=1, source_target_pairs={{0,1},{1,2},{2,3},{3,4},{4,5},{5,6},{6,7},{7,0},{8,9},{9,10},{10,1... | collective-permute-start | bytes 393224 | tf_op jit(solution)/shard_map/while/body/eval_jaxpr/ppermute | solution.py:21
  210.0 1.9 copy-start
  218.1 12.5 %collective-permute-start = (bf16[16,4096]{1,0:T(8,128)(2,1)S(1)}, bf16[16,4096]{1,0:T(8,128)(2,1)S(1)}, u32[]{:S(2)}, u32[]{:S(2)}) collective-permute-start(bf16[16,4096]{1,0:T(8,128)(2,1)S(1)} %copy.105), channel_id=1, source_target_pairs={{0,1},{1,2},{2,3},{3,4},{4,5},{5,6},{6,7},{7,0},{8,9},{9,10},{10,1... | collective-permute-start | bytes 393224 | tf_op jit(solution)/shard_map/while/body/eval_jaxpr/ppermute | solution.py:21
  222.5 1.9 copy-start
  230.7 14.2 %collective-permute-start = (bf16[16,4096]{1,0:T(8,128)(2,1)S(1)}, bf16[16,4096]{1,0:T(8,128)(2,1)S(1)}, u32[]{:S(2)}, u32[]{:S(2)}) collective-permute-start(bf16[16,4096]{1,0:T(8,128)(2,1)S(1)} %copy.105), channel_id=1, source_target_pairs={{0,1},{1,2},{2,3},{3,4},{4,5},{5,6},{6,7},{7,0},{8,9},{9,10},{10,1... | collective-permute-start | bytes 393224 | tf_op jit(solution)/shard_map/while/body/eval_jaxpr/ppermute | solution.py:21
  236.7 1.9 copy-start
  250.1 12.0 %all-to-all-start.2 = ((f32[8,1,512]{2,1,0:T(1,128)}), f32[8,1,512]{2,1,0:T(1,128)S(1)}, u32[]{:S(2)}, u32[]{:S(2)}) async-start(f32[8,1,512]{2,1,0:T(1,128)} %reshape.451), calls=%async_computation.2 | async-start | bytes 32768 | tf_op jit(solution)/shard_map/all_to_all | solution.py:151
  262.0 14.8 %all-to-all-start.3 = ((f32[8,1,512]{2,1,0:T(1,128)}), f32[8,1,512]{2,1,0:T(1,128)S(1)}, u32[]{:S(2)}, u32[]{:S(2)}) async-start(f32[8,1,512]{2,1,0:T(1,128)} %reshape.449), calls=%async_computation.3 | async-start | bytes 32768 | tf_op jit(solution)/shard_map/all_to_all | solution.py:152
  276.8 28.7 %all-to-all-start.1 = ((f32[8,16,4096]{2,1,0:T(8,128)}), f32[8,16,4096]{2,1,0:T(8,128)S(1)}, u32[]{:S(2)}, u32[]{:S(2)}) async-start(f32[8,16,4096]{2,1,0:T(8,128)} %constant_dynamic-update-slice_fusion.5), calls=%async_computation.1 | async-start | bytes 4194304 | tf_op jit(solution)/shard_map/all_to_all | solution.py:150
where the time goes:
time: 309 us; the launch traced here: 308 us
  waiting for transfers between devices  118 us (38%)
  matrix products  61.1 us (20%)
  local copies, waits for them, and re-layouts  58.1 us (19%)
  starting transfers between devices  41.5 us (13%)
  other arithmetic  28 us (9%)
    all_to_all x1, waiting for transfers between devices, local(): lax.all_to_all(outgoing, 'req', split_axis=0, concat_axis=0, tiled=True)  92.4 us
    dot_general x8, matrix products, attend(): jnp.einsum('kgrs,skd->rkgd', rounded, value_part, preferred_element_type=...  31.2 us
    dot_general x8, matrix products, attend(): jnp.einsum('rkgd,skd->kgrs', query_rows, key_part, preferred_element_type...  22 us
    all_to_all x1, waiting for transfers between devices, local(): lax.all_to_all(out_parts, 'ctx', split_axis=0, concat_axis=0, tiled=True)  18.1 us
    ppermute x7, starting transfers between devices, passed_along(): return lax.ppermute(value, axis, pairs)  16.6 us
    while x28, local copies, waits for them, and re-layouts  13.7 us
    reduce_sum x8, other arithmetic, attend(): block_total = jnp.sum(weights, axis=-1)  11.5 us
    all_to_all x1, starting transfers between devices, local(): lax.all_to_all(outgoing, 'req', split_axis=0, concat_axis=0, tiled=True)  9.94 us
  transfers between devices with their start and end apart: 11, of which 4 were waited for; matrix products, arithmetic and copies ran while one was open for 27% of the time, Pallas kernels for 0%

commit v1 on v0

v1 whole, which is shorter than its diff:
```python
import functools
import math

import jax
import jax.numpy as jnp
from jax import lax
from jax.experimental import pallas as pl
from jax.experimental.pallas import tpu as pltpu
from jax.sharding import PartitionSpec as P

QHEADS = 32
KVHEADS = 4
HEAD = 128
TILE = 8
GROUPS = QHEADS // KVHEADS
FEATURE = KVHEADS * HEAD
THETA = 500000.0
NEG = -1e30
FLOOR = -1e6
SCALE = math.log2(math.e) / math.sqrt(HEAD)
LANES = 128
WIDE = GROUPS * HEAD
CHUNKS = ((0, 3), (3, 1))
ANY = pl.BlockSpec(memory_space=pl.ANY)
VMEM = pl.BlockSpec(memory_space=pltpu.VMEM)
SMEM = pl.BlockSpec(memory_space=pltpu.SMEM)


def rotary(values, position, head_count):
    number = values.shape[0]
    half_size = HEAD // 2
    frequency = jnp.exp(-(2.0 * jnp.arange(half_size, dtype=jnp.float32) / HEAD) * math.log(THETA))
    angles = position.astype(jnp.float32)[:, None] * frequency[None, :]
    cosine = jnp.cos(angles)[:, None, :]
    sine = jnp.sin(angles)[:, None, :]
    shaped = values.astype(jnp.float32).reshape(number, head_count, HEAD)
    first_half = shaped[..., :half_size]
    second_half = shaped[..., half_size:]
    turned = jnp.concatenate(
        [first_half * cosine - second_half * sine, second_half * cosine + first_half * sine],
        axis=-1,
    )
    return turned.reshape(number, head_count * HEAD)


def pack_kernel(slot_ref, pages_ref, *refs):
    count = len(CHUNKS)
    outs, held, in_sem, out_sem = refs[:count], refs[count], refs[count + 1], refs[count + 2]
    pages = pages_ref.shape[0]
    load = pltpu.make_async_copy(pages_ref, held, in_sem)
    load.start()
    load.wait()
    for number, (start, heads) in enumerate(CHUNKS):
        width = heads * HEAD

        def send(owner, carry):
            slot = slot_ref[owner]
            for part in range(2):
                pltpu.make_async_copy(
                    held.at[slot, :, pl.ds(part * FEATURE + start * HEAD, width)],
                    outs[number].at[owner, :, pl.ds(part * width, width)],
                    out_sem.at[number],
                ).start()
            return carry

        lax.fori_loop(0, pages, send, 0)
    for number in range(count):
        pltpu.make_async_copy(outs[number], outs[number], out_sem.at[number]).wait()


def pack(slots, pages):
    count, page_len, _ = pages.shape
    shapes = [
        jax.ShapeDtypeStruct((count, page_len, 2 * heads * HEAD), jnp.bfloat16)
        for _, heads in CHUNKS
    ]
    return pl.pallas_call(
        pack_kernel,
        out_shape=shapes,
        in_specs=[SMEM, ANY],
        out_specs=[ANY] * len(CHUNKS),
        scratch_shapes=[
            pltpu.VMEM(pages.shape, jnp.bfloat16),
            pltpu.SemaphoreType.DMA,
            pltpu.SemaphoreType.DMA((len(CHUNKS),)),
        ],
        compiler_params=pltpu.CompilerParams(vmem_limit_bytes=16 << 20),
        cost_estimate=pl.CostEstimate(flops=0, transcendentals=0, bytes_accessed=16 << 20),
        name="pack",
    )(slots, pages)


BLOCK = 4


def attend_kernel(
    start, heads, store_ref, idx_ref, arrived_ref, fresh_ref, query_ref, pick_ref, bias_ref,
    old_ref, joined_ref, part_ref, held, keys, load_sem, save_sem,
):
    width = heads * HEAD
    pages, page_len = arrived_ref.shape[:2]
    span = pages * page_len
    rows = query_ref.shape[1]
    shards = query_ref.shape[0]

    def fetch(page, carry):
        pltpu.make_async_copy(
            arrived_ref.at[store_ref[page]],
            held.at[pl.ds(pl.multiple_of(page * page_len, page_len), page_len)],
            load_sem,
        ).start()
        return carry

    lax.fori_loop(0, pages, fetch, 0)
    keys[:, HEAD:] = bias_ref[...]
    pltpu.make_async_copy(held, held, load_sem).wait()

    for row in range(rows):
        place = idx_ref[row]
        base = pl.multiple_of((place // 16) * 16, 16)
        window = held[pl.ds(base, 16), :]
        hit = lax.broadcasted_iota(jnp.int32, window.shape, 0) == place - base
        fresh = jnp.concatenate(
            [
                fresh_ref[row : row + 1, start * HEAD : start * HEAD + width],
                fresh_ref[row : row + 1, FEATURE + start * HEAD : FEATURE + start * HEAD + width],
            ],
            axis=1,
        )
        held[pl.ds(base, 16), :] = jnp.where(
            hit, fresh.astype(jnp.float32), window.astype(jnp.float32)
        ).astype(jnp.bfloat16)

    saves = []
    for part in range(2):
        save = pltpu.make_async_copy(
            held.at[:, pl.ds(part * width, width)],
            joined_ref.at[0, :, pl.ds(part * FEATURE + start * HEAD, width)],
            save_sem.at[part],
        )
        save.start()
        saves.append(save)

    lane = lax.broadcasted_iota(jnp.int32, (rows, LANES), 1)

    def split(value):
        high = value.astype(jnp.bfloat16)
        rest = value - high.astype(jnp.float32)
        middle = rest.astype(jnp.bfloat16)
        low = (rest - middle.astype(jnp.float32)).astype(jnp.bfloat16)
        return [part.astype(jnp.float32) for part in (high, middle, low)]

    for head in range(heads):
        keys[:, :HEAD] = held[:, head * HEAD : (head + 1) * HEAD]

        def block(number, carry):
            tiles = []
            for inner in range(BLOCK):
                shard = number * BLOCK + inner
                pick = pick_ref[shard]
                for group in range(GROUPS):
                    column = head * WIDE + group * HEAD
                    tiles.append(
                        jnp.concatenate(
                            [query_ref[shard, :, column : column + HEAD], pick], axis=1
                        )
                    )
            query = jnp.concatenate(tiles, axis=0)
            scores = lax.dot_general(
                query, keys[...], (((1,), (1,)), ((), ())), preferred_element_type=jnp.float32
            )
            top = jnp.maximum(jnp.max(scores, axis=1, keepdims=True), FLOOR)
            weights = jnp.exp2((scores - top) * SCALE)
            total = jnp.sum(weights, axis=1, keepdims=True)
            mixed = lax.dot_general(
                weights.astype(jnp.bfloat16),
                held[:, width + head * HEAD : width + (head + 1) * HEAD],
                (((1,), (0,)), ((), ())),
                preferred_element_type=jnp.float32,
            ).astype(jnp.bfloat16)
            for inner in range(BLOCK):
                shard = number * BLOCK + inner
                stats = jnp.zeros((rows, LANES), jnp.float32)
                tops = jnp.zeros((rows, LANES), jnp.float32)
                totals = jnp.zeros((rows, LANES), jnp.float32)
                for group in range(GROUPS):
                    first = (inner * GROUPS + group) * rows
                    column = head * WIDE + group * HEAD
                    part_ref[shard, :, column : column + HEAD] = mixed[first : first + rows]
                    mine = lane % GROUPS == group
                    tops = jnp.where(mine, top[first : first + rows], tops)
                    totals = jnp.where(mine, total[first : first + rows], totals)
                for place, piece in enumerate(split(tops) + split(totals)):
                    stats = jnp.where(lane // GROUPS == place, piece, stats)
                part_ref[shard, :, heads * WIDE + head * LANES : heads * WIDE + (head + 1) * LANES] = (
                    stats.astype(jnp.bfloat16)
                )
            return carry

        lax.fori_loop(0, shards // BLOCK, block, 0)
    for save in saves:
        save.wait()


def attend(chunk, store, idx, arrived, fresh, query, pick, bias, joined):
    start, heads = chunk
    pages, page_len, width = arrived.shape
    span = pages * page_len
    shards, rows, _ = query.shape
    operands = [store, idx, arrived, fresh, query, pick, bias]
    specs = [
        SMEM,
        SMEM,
        ANY,
        VMEM,
        pl.BlockSpec((shards, rows, heads * WIDE), lambda i: (0, 0, start // heads)),
        VMEM,
        VMEM,
    ]
    aliases = {}
    if joined is not None:
        operands.append(joined)
        specs.append(ANY)
        aliases = {len(operands) - 1: 0}
        body = functools.partial(attend_kernel, start, heads)
    else:
        def body(*refs):
            attend_kernel(start, heads, *refs[:7], None, *refs[7:])

    work = shards * rows * GROUPS * heads * span
    return pl.pallas_call(
        body,
        grid=(1,),
        out_shape=[
            jax.ShapeDtypeStruct((1, span, 2 * FEATURE), jnp.bfloat16),
            jax.ShapeDtypeStruct((shards, rows, heads * (WIDE + LANES)), jnp.bfloat16),
        ],
        in_specs=specs,
        out_specs=[ANY, VMEM],
        scratch_shapes=[
            pltpu.VMEM((span, width), jnp.bfloat16),
            pltpu.VMEM((span, 2 * HEAD), jnp.bfloat16),
            pltpu.SemaphoreType.DMA,
            pltpu.SemaphoreType.DMA((2,)),
        ],
        input_output_aliases=aliases,
        compiler_params=pltpu.CompilerParams(vmem_limit_bytes=40 << 20),
        cost_estimate=pl.CostEstimate(
            flops=work * 512, transcendentals=work, bytes_accessed=span * width * 4
        ),
        name="attend",
    )(*operands)


def merge_kernel(heads, part_ref, *refs):
    out_ref = refs[-1]
    shards, rows, _ = part_ref.shape
    for head in range(heads):
        column = heads * WIDE + head * LANES
        tops, totals = [], []
        for shard in range(shards):
            stats = part_ref[shard, :, column : column + LANES].astype(jnp.float32)
            moved = [stats] + [
                pltpu.roll(stats, LANES - GROUPS * place, 1) for place in range(1, 6)
            ]
            tops.append(moved[0] + moved[1] + moved[2])
            totals.append(moved[3] + moved[4] + moved[5])
        best = functools.reduce(jnp.maximum, tops)
        factors = [jnp.exp2((top - best) * SCALE) for top in tops]
        whole = sum(factor * total for factor, total in zip(factors, totals))
        shares = [factor / whole for factor in factors]
        for group in range(GROUPS):
            first = head * WIDE + group * HEAD
            out_ref[0, :, first : first + HEAD] = sum(
                part_ref[shard, :, first : first + HEAD].astype(jnp.float32)
                * shares[shard][:, group : group + 1]
                for shard in range(shards)
            ).astype(jnp.bfloat16)


def merge(chunk, part, attended):
    start, heads = chunk
    shards, rows, _ = part.shape
    operands, specs, aliases = [part], [VMEM], {}
    if attended is not None:
        operands.append(attended)
        specs.append(ANY)
        aliases = {1: 0}
    return pl.pallas_call(
        functools.partial(merge_kernel, heads),
        grid=(1,),
        out_shape=jax.ShapeDtypeStruct((1, rows, QHEADS * HEAD), jnp.bfloat16),
        in_specs=specs,
        out_specs=pl.BlockSpec((1, rows, heads * WIDE), lambda i: (0, 0, start // heads)),
        input_output_aliases=aliases,
        cost_estimate=pl.CostEstimate(
            flops=shards * rows * heads * WIDE * 2, transcendentals=0, bytes_accessed=1 << 20
        ),
        name="merge",
    )(*operands)


def local(
    queries, fresh_kv, cache_pages, stretch_store, stretch_request, recompute_idx, block_mask
):
    shards = lax.axis_size("ctx")
    device = lax.axis_index("ctx")
    stores = lax.axis_size("req")
    pages, page_len = cache_pages.shape[2:4]
    span = pages * page_len
    rows = queries.shape[1]
    tiles = rows // TILE

    targets = stretch_request[0, 0]
    order = jnp.arange(stores, dtype=jnp.int32)
    slots = jnp.sum(
        jnp.where(order[:, None] == targets[None, :], jnp.arange(pages, dtype=jnp.int32)[None, :], 0),
        axis=1,
        dtype=jnp.int32,
    )
    packed = pack(slots, cache_pages[0, 0])

    own_idx = lax.dynamic_index_in_dim(recompute_idx[0], device, 0, keepdims=False)
    own_pos = device * span + own_idx
    rotated = rotary(queries[0], own_pos, QHEADS).astype(jnp.bfloat16)
    query = lax.all_gather(rotated, "ctx", axis=0)
    fresh_rows = fresh_kv[0]
    fresh = jnp.concatenate(
        [rotary(fresh_rows[:, :FEATURE], own_pos, KVHEADS), fresh_rows[:, FEATURE:].astype(jnp.float32)],
        axis=1,
    ).astype(jnp.bfloat16)

    mask_cols = lax.dynamic_index_in_dim(block_mask[0], device, 2, keepdims=False) == 1
    shard_ids = jnp.arange(shards, dtype=jnp.int32)
    far = (mask_cols & (shard_ids > device)[:, None, None]).reshape(shards * tiles, pages)
    own_mask = lax.dynamic_index_in_dim(mask_cols, device, 0, keepdims=False)
    page_ids = jnp.arange(pages, dtype=jnp.int32)
    near = jnp.repeat(own_mask, TILE, axis=0) | (page_ids[None, :] == (own_idx // page_len)[:, None])
    spare = LANES - shards * tiles - rows
    allowed = jnp.concatenate([far, near, jnp.ones((spare, pages), bool)], axis=0).T
    limit = jnp.concatenate(
        [
            jnp.full((shards * tiles,), span, jnp.int32),
            own_idx,
            jnp.full((spare,), span, jnp.int32),
        ]
    )
    key_ids = jnp.arange(span, dtype=jnp.int32).reshape(pages, page_len)
    bias = jnp.where(
        allowed[:, None, :] & (key_ids[:, :, None] <= limit[None, None, :]), 0.0, NEG
    ).astype(jnp.bfloat16).reshape(span, LANES)
    row_ids = jnp.arange(rows, dtype=jnp.int32)
    column = jnp.where(
        (shard_ids == device)[:, None],
        shards * tiles + row_ids[None, :],
        shard_ids[:, None] * tiles + row_ids[None, :] // TILE,
    )
    pick = (column[:, :, None] == jnp.arange(LANES, dtype=jnp.int32)).astype(jnp.bfloat16)

    joined = attended = None
    for number, chunk in enumerate(CHUNKS):
        arrived = lax.all_to_all(packed[number], "req", split_axis=0, concat_axis=0, tiled=True)
        joined, part = attend(
            chunk, stretch_store[0, 0], own_idx, arrived, fresh, query, pick, bias, joined
        )
        part = lax.all_to_all(part, "ctx", split_axis=0, concat_axis=0, tiled=True)
        attended = merge(chunk, part, attended)
    return attended, joined


def solution(mesh):
    return jax.shard_map(
        local,
        mesh=mesh,
        in_specs=(
            P("req", "ctx", None),
            P("req", "ctx", None),
            P("req", "ctx", None, None, None),
            P("req", "ctx", None),
            P("req", "ctx", None),
            P("req", None, None),
            P("req", None, None, None, None),
        ),
        out_specs=(P("req", "ctx", None), P("req", "ctx", None)),
        check_vma=False,
    )
```

time: 309 us -> 177 us (0.57)
  matrix products: 61.1 us -> 0 us
  local copies, waits for them, and re-layouts: 58.1 us -> 11.6 us
  Pallas kernels: 0 us -> 39.3 us
  waiting for transfers between devices: 118 us -> 81.1 us
  other arithmetic: 28 us -> 3.79 us
  starting transfers between devices: 41.5 us -> 25.7 us
  between operations: 0.98 us -> 14.3 us
    dot_general x17 -> x0, matrix products: 61.1 us -> none  [the longest x8 31.2 us: attend(): jnp.einsum('kgrs,skd->rkgd', rounded, value_part, preferred_element_type=...]
    pallas_call x0 -> x5, Pallas kernels: none -> 39.3 us  [the longest x2 32.2 us: attend(): pl.pallas_call(body, grid=(1,), out_shape=[jax.ShapeDtypeStruct((1, span,...]
    all_to_all x4, waiting for transfers between devices: 118 us -> 81.1 us  [the longest x2 70.1 us: local(): lax.all_to_all(packed[number], 'req', split_axis=0, concat_axis=0, tiled=...]
    ppermute x7 -> x0, starting transfers between devices: 16.6 us -> none  [passed_along(): return lax.ppermute(value, axis, pairs)]
    while x28 -> x0, local copies, waits for them, and re-layouts: 13.7 us -> none
    reduce_sum x10 -> x1, other arithmetic: 13.4 us -> 0.77 us  [local(): jnp.sum(jnp.where(order[:, None] == targets[None, :], jnp.arange(pages, d...]
    slice x3 -> x0, local copies, waits for them, and re-layouts: 10.3 us -> none  [the longest x2 7.34 us: local(): value_rows = joined_rows[:, feature:].reshape(span_len, KVHEADS, HEAD)]
    dynamic_update_slice x38 -> x0, local copies, waits for them, and re-layouts: 6.84 us -> none  [the longest x8 5.83 us: place(): lax.dynamic_update_slice(out_parts, mixture[None], (source, zero_index, j...]
  transfers between devices with their start and end apart: 11 -> 5, of which waited for: 4 -> 4; matrix products, arithmetic and copies ran while one was open for 27% -> 2% of each run, Pallas kernels for 0% -> 20%
where the time goes in v1:
time: 177 us; the launch traced here: 176 us
  waiting for transfers between devices  81.1 us (46%)
  Pallas kernels  39.3 us (22%)
  starting transfers between devices  25.7 us (15%)
  between operations  14.3 us (8%)
  local copies, waits for them, and re-layouts  11.6 us (7%)
  other arithmetic  3.79 us (2%)
    all_to_all x2, waiting for transfers between devices, local(): lax.all_to_all(packed[number], 'req', split_axis=0, concat_axis=0, tiled=...  70.1 us
    pallas_call x2, Pallas kernels, attend(): pl.pallas_call(body, grid=(1,), out_shape=[jax.ShapeDtypeStruct((1, span,...  32.2 us
    all_to_all x2, starting transfers between devices, local(): lax.all_to_all(packed[number], 'req', split_axis=0, concat_axis=0, tiled=...  15 us
    all_to_all x2, waiting for transfers between devices, local(): part = lax.all_to_all(part, 'ctx', split_axis=0, concat_axis=0, tiled=True)  11 us
    all_to_all x2, starting transfers between devices, local(): part = lax.all_to_all(part, 'ctx', split_axis=0, concat_axis=0, tiled=True)  10.7 us
    unnamed x25, local copies, waits for them, and re-layouts  10.4 us
    pallas_call x2, Pallas kernels, merge(): pl.pallas_call(functools.partial(merge_kernel, heads), grid=(1,), out_sha...  4.85 us
  transfers between devices with their start and end apart: 5, of which 4 were waited for; matrix products, arithmetic and copies ran while one was open for 2% of the time, Pallas kernels for 20%

profile of v1, /device:TPU:32, one launch (start us, length us, event | category | flops | bytes accessed | tf_op | source)
XLA Modules:
  0.0 175.8 jit_solution(12116983460472807466)
XLA Ops:
  7.2 0.8 select_reduce_fusion.slot_ref
  7.9 2.2 %copy-done = bf16[1,1,32,64,1024]{4,3,2,1,0:T(8,128)(2,1)S(1)} copy-done((bf16[1,1,32,64,1024]{4,3,2,1,0:T(8,128)(2,1)S(1)}, bf16[1,1,32,64,1024]{4,3,2,1,0:T(8,128)(2,1)}, u32[]{:S(2)}) %copy-start) | copy-done | bytes 4194328
  10.1 2.3 %pack.1 = (bf16[32,64,768]{2,1,0:T(8,128)(2,1)S(1)}, bf16[32,64,256]{2,1,0:T(8,128)(2,1)S(1)}) custom-call(s32[32]{0:T(128)S(1)} %select_reduce_fusion.slot_ref, bf16[32,64,1024]{2,1,0:T(8,128)(2,1)S(1)} %bitcast.26), custom_call_target="tpu_custom_call" | custom-call | bytes 16777216 | tf_op jit(solution)/shard_map/pack/pallas_call | solution.py:77
  12.4 0.0 copy-start.3
  12.4 1.7 copy-done.3
  14.1 0.9 copy-done.4
  15.0 9.9 %all-to-all-start.1 = ((bf16[32,64,768]{2,1,0:T(8,128)(2,1)}), bf16[32,64,768]{2,1,0:T(8,128)(2,1)S(1)}, u32[]{:S(2)}, u32[]{:S(2)}) async-start(bf16[32,64,768]{2,1,0:T(8,128)(2,1)} %copy-done.3), calls=%async_computation.1 | async-start | bytes 6291456 | tf_op jit(solution)/shard_map/all_to_all | solution.py:362
  24.9 0.0 copy-start.7
  24.9 0.0 all-gather.2.cloned.1.call-start
  25.0 0.1 copy.22
  25.1 0.7 and_select_fusion
  25.8 0.1 multiply_cosine_fusion
  25.9 0.1 subtract_convert_fusion
  26.1 0.1 pad_maximum_fusion
  26.2 0.7 convert_element_type.39
  26.9 0.0 all-gather.2.cloned.1.call-update
  26.9 0.1 and.54
  27.0 0.1 and.55
  27.1 0.9 fusion.3
  28.0 0.1 broadcast_and_fusion
  28.1 0.1 fusion.1
  28.2 69.7 %all-to-all-done.1.refs_2_ = bf16[32,64,768]{2,1,0:T(8,128)(2,1)S(1)} async-done(((bf16[32,64,768]{2,1,0:T(8,128)(2,1)}), bf16[32,64,768]{2,1,0:T(8,128)(2,1)S(1)}, u32[]{:S(2)}, u32[]{:S(2)}) %all-to-all-start.1) | async-done | bytes 3145760 | tf_op jit(solution)/shard_map/all_to_all | solution.py:362
  97.9 1.7 copy-done.1
  99.5 5.1 %all-to-all-start = ((bf16[32,64,256]{2,1,0:T(8,128)(2,1)}), bf16[32,64,256]{2,1,0:T(8,128)(2,1)S(1)}, u32[]{:S(2)}, u32[]{:S(2)}) async-start(bf16[32,64,256]{2,1,0:T(8,128)(2,1)} %copy-done.4), calls=%async_computation | async-start | bytes 2097152 | tf_op jit(solution)/shard_map/all_to_all | solution.py:362
  104.7 0.1 copy.18
  104.8 0.1 copy.17
  104.9 0.1 broadcast_in_dim_reshape.12
  105.0 0.1 subtract_convert_fusion.1
  105.1 0.1 pad_maximum_fusion.2
  105.2 0.1 pad.5.clone
  105.3 0.1 pad_add_fusion
  105.3 0.1 add_bitcast_fusion
  105.4 0.3 select_convert_fusion.refs_6_.bias_ref
  105.8 0.1 add_select_fusion
  105.9 0.1 fusion.refs_5_.pick_ref
  106.0 0.0 all-gather.2.cloned.1.call-done.refs_4_.query_ref
  106.0 1.9 %copy-done.2 = bf16[32,64,768]{2,1,0:T(8,128)(2,1)S(1)} copy-done((bf16[32,64,768]{2,1,0:T(8,128)(2,1)S(1)}, bf16[32,64,768]{2,1,0:T(8,128)(2,1)}, u32[]{:S(2)}) %copy-start.2) | copy-done | bytes 3145752
  107.9 1.2 copy-done.5
  109.1 23.3 %attend.2 = (bf16[1,2048,1024]{2,1,0:T(8,128)(2,1)}, bf16[8,16,3456]{2,1,0:T(8,128)(2,1)}) custom-call(s32[32]{0:T(128)S(1)} %bitcast.27, s32[16]{0:T(128)S(1)} %get-tuple-element.17.refs_1_.idx_ref, bf16[32,64,768]{2,1,0:T(8,128)(2,1)S(1)} %copy-done.2, bf16[16,1024]{1,0:T(8,128)(2,1)S(1)} %pad_maximum_fusion.1.refs_3_.fresh_ref, ...), custom_call_target="tpu_custom_call" | custom-call | flops 3221225472 | bytes 6291456 | tf_op jit(solution)/shard_map/attend/pallas_call | solution.py:231
  132.4 0.4 all-to-all-done.arrived_ref
  132.8 6.6 %all-to-all-start.3 = ((bf16[8,16,3456]{2,1,0:T(8,128)(2,1)}), bf16[8,16,3456]{2,1,0:T(8,128)(2,1)}, u32[]{:S(2)}, u32[]{:S(2)}) async-start(bf16[8,16,3456]{2,1,0:T(8,128)(2,1)} %get-tuple-element.12), calls=%async_computation.3 | async-start | bytes 1769472 | tf_op jit(solution)/shard_map/all_to_all | solution.py:366
  139.5 8.9 %attend.3 = (bf16[1,2048,1024]{2,1,0:T(8,128)(2,1)}, bf16[8,16,1152]{2,1,0:T(8,128)(2,1)}) custom-call(s32[32]{0:T(128)S(1)} %bitcast.28, s32[16]{0:T(128)S(1)} %get-tuple-element.17.refs_1_.idx_ref, bf16[32,64,256]{2,1,0:T(8,128)(2,1)S(1)} %all-to-all-done.arrived_ref, ...), custom_call_target="tpu_custom_call", output_to_operand_aliasing={{0}: (7, {})} | custom-call | flops 1073741824 | bytes 2097152 | tf_op jit(solution)/shard_map/attend/pallas_call | solution.py:231
  148.3 5.4 %all-to-all-done.3.part_ref = bf16[8,16,3456]{2,1,0:T(8,128)(2,1)} async-done(((bf16[8,16,3456]{2,1,0:T(8,128)(2,1)}), bf16[8,16,3456]{2,1,0:T(8,128)(2,1)}, u32[]{:S(2)}, u32[]{:S(2)}) %all-to-all-start.3) | async-done | bytes 884768 | tf_op jit(solution)/shard_map/all_to_all | solution.py:366
  153.7 4.0 %all-to-all-start.2 = ((bf16[8,16,1152]{2,1,0:T(8,128)(2,1)}), bf16[8,16,1152]{2,1,0:T(8,128)(2,1)S(1)}, u32[]{:S(2)}, u32[]{:S(2)}) async-start(bf16[8,16,1152]{2,1,0:T(8,128)(2,1)} %get-tuple-element.11), calls=%async_computation.2 | async-start | bytes 589824 | tf_op jit(solution)/shard_map/all_to_all | solution.py:366
  157.7 2.9 %merge.2.refs_0_ = bf16[1,16,4096]{2,1,0:T(8,128)(2,1)} custom-call(bf16[8,16,3456]{2,1,0:T(8,128)(2,1)} %all-to-all-done.3.part_ref), custom_call_target="tpu_custom_call" | custom-call | flops 786432 | bytes 1048576 | tf_op jit(solution)/shard_map/merge/pallas_call | solution.py:289
  160.7 5.7 %all-to-all-done.2.part_ref = bf16[8,16,1152]{2,1,0:T(8,128)(2,1)S(1)} async-done(((bf16[8,16,1152]{2,1,0:T(8,128)(2,1)}), bf16[8,16,1152]{2,1,0:T(8,128)(2,1)S(1)}, u32[]{:S(2)}, u32[]{:S(2)}) %all-to-all-start.2) | async-done | bytes 294944 | tf_op jit(solution)/shard_map/all_to_all | solution.py:366
  166.3 0.7 copy-done.8
  167.0 1.9 %merge.3 = bf16[1,16,4096]{2,1,0:T(8,128)(2,1)} custom-call(bf16[8,16,1152]{2,1,0:T(8,128)(2,1)} %copy-done.8, bf16[1,16,4096]{2,1,0:T(8,128)(2,1)} %merge.2.refs_0_), custom_call_target="tpu_custom_call", output_to_operand_aliasing={{}: (1, {})} | custom-call | flops 262144 | bytes 1048576 | tf_op jit(solution)/shard_map/merge/pallas_call | solution.py:289
  (30 shorter events, 0.2 us)
Async XLA Ops:
  7.9 2.2 %copy-start = (bf16[1,1,32,64,1024]{4,3,2,1,0:T(8,128)(2,1)S(1)}, bf16[1,1,32,64,1024]{4,3,2,1,0:T(8,128)(2,1)}, u32[]{:S(2)}) copy-start(bf16[1,1,32,64,1024]{4,3,2,1,0:T(8,128)(2,1)} %param.9) | copy-start | bytes 12582916
  12.4 1.7 copy-start.3
  14.1 0.9 copy-start.4
  15.0 10.0 %copy-start.9 = (bf16[1,16,4096]{2,1,0:T(8,128)(2,1)S(1)}, bf16[1,16,4096]{2,1,0:T(8,128)(2,1)}, u32[]{:S(2)}) copy-start(bf16[1,16,4096]{2,1,0:T(8,128)(2,1)} %param.7) | copy-start | bytes 393220
  15.0 89.9 %copy-start.10 = (bf16[1,16,1024]{2,1,0:T(8,128)(2,1)S(1)}, bf16[1,16,1024]{2,1,0:T(8,128)(2,1)}, u32[]{:S(2)}) copy-start(bf16[1,16,1024]{2,1,0:T(8,128)(2,1)} %param.8) | copy-start | bytes 98308
  15.0 82.9 %all-to-all-start.1 = ((bf16[32,64,768]{2,1,0:T(8,128)(2,1)}), bf16[32,64,768]{2,1,0:T(8,128)(2,1)S(1)}, u32[]{:S(2)}, u32[]{:S(2)}) async-start(bf16[32,64,768]{2,1,0:T(8,128)(2,1)} %copy-done.3), calls=%async_computation.1 | async-start | bytes 6291456 | tf_op jit(solution)/shard_map/all_to_all | solution.py:362
  24.9 81.1 %copy-start.7 = (s32[1,1,32]{2,1,0:T(1,128)S(1)}, s32[1,1,32]{2,1,0:T(1,128)}, u32[]{:S(2)}) copy-start(s32[1,1,32]{2,1,0:T(1,128)} %param.10) | copy-start | bytes 388
  24.9 81.1 %all-gather.2.cloned.1.call-start = ((), (), s32[]{:S(2)}) async-start(), calls=%async_computation.4 | async-start | bytes 1179648 | tf_op jit(solution)/shard_map/all_gather | solution.py:326
  97.9 1.7 copy-start.1
  99.5 33.3 %all-to-all-start = ((bf16[32,64,256]{2,1,0:T(8,128)(2,1)}), bf16[32,64,256]{2,1,0:T(8,128)(2,1)S(1)}, u32[]{:S(2)}, u32[]{:S(2)}) async-start(bf16[32,64,256]{2,1,0:T(8,128)(2,1)} %copy-done.4), calls=%async_computation | async-start | bytes 2097152 | tf_op jit(solution)/shard_map/all_to_all | solution.py:362
  106.0 1.9 %copy-start.2 = (bf16[32,64,768]{2,1,0:T(8,128)(2,1)S(1)}, bf16[32,64,768]{2,1,0:T(8,128)(2,1)}, u32[]{:S(2)}) copy-start(bf16[32,64,768]{2,1,0:T(8,128)(2,1)} %copy-done.1) | copy-start | bytes 9437188
  107.9 1.2 copy-start.5
  109.1 30.3 %copy-start.6 = (bf16[8,16,4096]{2,1,0:T(8,128)(2,1)S(1)}, bf16[8,16,4096]{2,1,0:T(8,128)(2,1)}, u32[]{:S(2)}) copy-start(bf16[8,16,4096]{2,1,0:T(8,128)(2,1)} %all-gather.2.cloned.1.call-done.refs_4_.query_ref) | copy-start | bytes 3145732
  132.8 20.9 %all-to-all-start.3 = ((bf16[8,16,3456]{2,1,0:T(8,128)(2,1)}), bf16[8,16,3456]{2,1,0:T(8,128)(2,1)}, u32[]{:S(2)}, u32[]{:S(2)}) async-start(bf16[8,16,3456]{2,1,0:T(8,128)(2,1)} %get-tuple-element.12), calls=%async_computation.3 | async-start | bytes 1769472 | tf_op jit(solution)/shard_map/all_to_all | solution.py:366
  153.7 12.6 %all-to-all-start.2 = ((bf16[8,16,1152]{2,1,0:T(8,128)(2,1)}), bf16[8,16,1152]{2,1,0:T(8,128)(2,1)S(1)}, u32[]{:S(2)}, u32[]{:S(2)}) async-start(bf16[8,16,1152]{2,1,0:T(8,128)(2,1)} %get-tuple-element.11), calls=%async_computation.2 | async-start | bytes 589824 | tf_op jit(solution)/shard_map/all_to_all | solution.py:366
  166.3 0.7 copy-start.8
Sparse Core Ops, SparseCore 0:
  28.9 66.2 all-gather.1

commit v2 on v1

v2 whole, which is shorter than its diff:
```python
import functools
import math

import jax
import jax.numpy as jnp
from jax import lax
from jax.experimental import pallas as pl
from jax.experimental.pallas import tpu as pltpu
from jax.sharding import PartitionSpec as P

QHEADS = 32
KVHEADS = 4
HEAD = 128
TILE = 8
GROUPS = QHEADS // KVHEADS
FEATURE = KVHEADS * HEAD
THETA = 500000.0
NEG = -1e30
FLOOR = -1e6
SCALE = math.log2(math.e) / math.sqrt(HEAD)
LANES = 128
WIDE = GROUPS * HEAD
CHUNKS = ((0, 2), (2, 2))
ANY = pl.BlockSpec(memory_space=pl.ANY)
VMEM = pl.BlockSpec(memory_space=pltpu.VMEM)
SMEM = pl.BlockSpec(memory_space=pltpu.SMEM)
HBM = pl.BlockSpec(memory_space=pltpu.HBM)


def rotary(values, position, head_count):
    number = values.shape[0]
    half_size = HEAD // 2
    frequency = jnp.exp(-(2.0 * jnp.arange(half_size, dtype=jnp.float32) / HEAD) * math.log(THETA))
    angles = position.astype(jnp.float32)[:, None] * frequency[None, :]
    cosine = jnp.cos(angles)[:, None, :]
    sine = jnp.sin(angles)[:, None, :]
    shaped = values.astype(jnp.float32).reshape(number, head_count, HEAD)
    first_half = shaped[..., :half_size]
    second_half = shaped[..., half_size:]
    turned = jnp.concatenate(
        [first_half * cosine - second_half * sine, second_half * cosine + first_half * sine],
        axis=-1,
    )
    return turned.reshape(number, head_count * HEAD)


def ways(chunk):
    start, heads = chunk
    width = heads * HEAD
    return ((start * HEAD, width, 0), (FEATURE + start * HEAD, width, width))


def pack_kernel(chunk, slot_ref, pages_ref, out_ref, held, in_sem, out_sem):
    loads, saves = [], []
    for owner in range(pages_ref.shape[0]):
        for half, (start, width, column) in enumerate(ways(chunk)):
            load = pltpu.make_async_copy(
                pages_ref.at[slot_ref[owner], :, pl.ds(start, width)],
                held.at[owner, :, pl.ds(column, width)],
                in_sem.at[owner, half],
            )
            load.start()
            loads.append(load)
    for owner in range(pages_ref.shape[0]):
        loads[2 * owner].wait()
        loads[2 * owner + 1].wait()
        save = pltpu.make_async_copy(held.at[owner], out_ref.at[owner], out_sem.at[owner])
        save.start()
        saves.append(save)
    for save in saves:
        save.wait()


def pack(name, chunk, slots, pages):
    count, page_len, _ = pages.shape
    shape = (count, page_len, 2 * chunk[1] * HEAD)
    return pl.pallas_call(
        functools.partial(pack_kernel, chunk),
        out_shape=jax.ShapeDtypeStruct(shape, jnp.bfloat16),
        in_specs=[SMEM, HBM],
        out_specs=HBM,
        scratch_shapes=[
            pltpu.VMEM(shape, jnp.bfloat16),
            pltpu.SemaphoreType.DMA((count, 2)),
            pltpu.SemaphoreType.DMA((count,)),
        ],
        compiler_params=pltpu.CompilerParams(vmem_limit_bytes=60 << 20),
        cost_estimate=pl.CostEstimate(flops=0, transcendentals=0, bytes_accessed=8 << 20),
        name=name,
    )(slots, pages)


BLOCK = 2
KB = 512


def attend_kernel(
    start, heads, held_back, count, place_ref, order_ref, from_ref, idx_ref, fresh_ref,
    query_ref, pick_ref, bias_ref, *refs,
):
    arrived_ref, refs = refs[0], refs[held_back:]
    joined_ref, parts, (held, keys, scores_s, probs_s, load_sem, save_sem) = (
        refs[0], refs[1 : 1 + count], refs[1 + count :],
    )
    width = heads * HEAD
    span = bias_ref.shape[0]
    pages, page_len = arrived_ref.shape[:2]
    rows = query_ref.shape[1]
    shards = query_ref.shape[0]
    if count == 1:
        parts = [parts[0].at[shard] for shard in range(shards)]

    for source in range(pages):
        place = pl.ds(pl.multiple_of(place_ref[source] * page_len, page_len), page_len)
        pltpu.make_async_copy(arrived_ref.at[source], held.at[place], load_sem).start()
    keys[:, HEAD:] = bias_ref[...]
    pltpu.make_async_copy(held, held, load_sem).wait()

    for row in range(rows):
        place = idx_ref[row]
        base = pl.multiple_of((place // 16) * 16, 16)
        window = held[pl.ds(base, 16), :]
        hit = lax.broadcasted_iota(jnp.int32, window.shape, 0) == place - base
        fresh = jnp.concatenate(
            [
                fresh_ref[row : row + 1, start * HEAD : start * HEAD + width],
                fresh_ref[row : row + 1, FEATURE + start * HEAD : FEATURE + start * HEAD + width],
            ],
            axis=1,
        )
        held[pl.ds(base, 16), :] = jnp.where(
            hit, fresh.astype(jnp.float32), window.astype(jnp.float32)
        ).astype(jnp.bfloat16)

    saves = []
    for part in range(2):
        save = pltpu.make_async_copy(
            held.at[:, pl.ds(part * width, width)],
            joined_ref.at[0, :, pl.ds(part * FEATURE + start * HEAD, width)],
            save_sem.at[part],
        )
        save.start()
        saves.append(save)

    lane = lax.broadcasted_iota(jnp.int32, (rows, LANES), 1)

    def split(value):
        high = value.astype(jnp.bfloat16)
        rest = value - high.astype(jnp.float32)
        middle = rest.astype(jnp.bfloat16)
        low = (rest - middle.astype(jnp.float32)).astype(jnp.bfloat16)
        return [part.astype(jnp.float32) for part in (high, middle, low)]

    span_blocks = span // KB
    def lanes(start, size):
        return pl.ds(start if isinstance(start, int) else pl.multiple_of(start, LANES), size)

    def one_head(head, carry):
        keys[:, :HEAD] = held[:, lanes(head * HEAD, HEAD)]

        def first(number, slot):
            tiles = []
            for inner in range(BLOCK):
                shard = from_ref[number * BLOCK + inner]
                pick = pick_ref[order_ref[number * BLOCK + inner]]
                for group in range(GROUPS):
                    column = head * WIDE + group * HEAD
                    tiles.append(
                        jnp.concatenate(
                            [query_ref[shard, :, lanes(column, HEAD)], pick], axis=1
                        )
                    )
            query = jnp.concatenate(tiles, axis=0)
            top = None
            for kb in range(span_blocks):
                s = lax.dot_general(
                    query, keys[kb * KB : (kb + 1) * KB], (((1,), (1,)), ((), ())),
                    preferred_element_type=jnp.float32,
                )
                scores_s[slot, :, kb * KB : (kb + 1) * KB] = s
                for c in range(KB // LANES):
                    t = s[:, c * LANES : (c + 1) * LANES]
                    top = t if top is None else jnp.maximum(top, t)
            return jnp.maximum(jnp.max(top, axis=1, keepdims=True), FLOOR)

        def second(number, slot, top):
            total = None
            for c in range(span // LANES):
                p = jnp.exp2((scores_s[slot, :, c * LANES : (c + 1) * LANES] - top) * SCALE)
                total = p if total is None else total + p
                probs_s[slot, :, c * LANES : (c + 1) * LANES] = p.astype(jnp.bfloat16)
            total = jnp.sum(total, axis=1, keepdims=True)
            mixed = lax.dot_general(
                probs_s[slot],
                held[:, lanes(width + head * HEAD, HEAD)],
                (((1,), (0,)), ((), ())),
                preferred_element_type=jnp.float32,
            ).astype(jnp.bfloat16)
            for inner in range(BLOCK):
                shard = number * BLOCK + inner
                stats = jnp.zeros((rows, LANES), jnp.float32)
                tops = jnp.zeros((rows, LANES), jnp.float32)
                totals = jnp.zeros((rows, LANES), jnp.float32)
                for group in range(GROUPS):
                    first = (inner * GROUPS + group) * rows
                    column = head * WIDE + group * HEAD
                    parts[shard][:, lanes(column, HEAD)] = mixed[first : first + rows]
                    mine = lane % GROUPS == group
                    tops = jnp.where(mine, top[first : first + rows], tops)
                    totals = jnp.where(mine, total[first : first + rows], totals)
                for place, piece in enumerate(split(tops) + split(totals)):
                    stats = jnp.where(lane // GROUPS == place, piece, stats)
                parts[shard][:, lanes(heads * WIDE + head * LANES, LANES)] = (
                    stats.astype(jnp.bfloat16)
                )

        count = shards // BLOCK
        top = first(0, 0)
        for number in range(count):
            after = first(number + 1, (number + 1) % 2) if number + 1 < count else None
            second(number, number % 2, top)
            top = after
        return carry

    if count == 1:
        for head in range(heads):
            one_head(head, 0)
    else:
        lax.fori_loop(0, heads, one_head, 0)
    for save in saves:
        save.wait()


def attend(chunk, count, tables, arrived, fresh, query, pick, bias, joined, after=()):
    start, heads = chunk
    width = 2 * heads * HEAD
    span = bias.shape[0]
    shards, rows, _ = query.shape
    operands = list(tables) + [fresh, query, pick, bias, arrived]
    specs = [SMEM] * len(tables) + [
        VMEM,
        pl.BlockSpec((shards, rows, heads * WIDE), lambda i: (0, 0, start // heads)),
        VMEM,
        VMEM,
        HBM,
    ]
    aliases = {}
    if joined is not None:
        operands.append(joined)
        specs.append(HBM)
        aliases = {len(operands) - 1: 0}
    operands += after
    specs += [HBM] * len(after)
    across = heads * (WIDE + LANES)
    part = (rows, across) if count > 1 else (shards, rows, across)
    work = shards * rows * GROUPS * heads * span
    return pl.pallas_call(
        functools.partial(attend_kernel, start, heads, len(operands) - len(tables) - 4, count),
        grid=(1,),
        out_shape=[
            jax.ShapeDtypeStruct((1, span, 2 * FEATURE), jnp.bfloat16),
        ]
        + [jax.ShapeDtypeStruct(part, jnp.bfloat16)] * count,
        in_specs=specs,
        out_specs=[HBM] + [VMEM] * count,
        scratch_shapes=[
            pltpu.VMEM((span, width), jnp.bfloat16),
            pltpu.VMEM((span, 2 * HEAD), jnp.bfloat16),
            pltpu.VMEM((2, BLOCK * LANES, span), jnp.float32),
            pltpu.VMEM((2, BLOCK * LANES, span), jnp.bfloat16),
            pltpu.SemaphoreType.DMA,
            pltpu.SemaphoreType.DMA((2,)),
        ],
        input_output_aliases=aliases,
        compiler_params=pltpu.CompilerParams(vmem_limit_bytes=60 << 20),
        cost_estimate=pl.CostEstimate(
            flops=work * 5120, transcendentals=work, bytes_accessed=span * width * 4
        ),
        name="attend",
    )(*operands)


def merge_kernel(heads, count, *refs):
    parts, out_ref = refs[:count], refs[-1]
    if count == 1:
        parts = [parts[0].at[shard] for shard in range(parts[0].shape[0])]
    shards = len(parts)
    for head in range(heads):
        column = heads * WIDE + head * LANES
        tops, totals = [], []
        for shard in range(shards):
            stats = parts[shard][:, column : column + LANES].astype(jnp.float32)
            moved = [stats] + [
                pltpu.roll(stats, LANES - GROUPS * place, 1) for place in range(1, 6)
            ]
            tops.append(moved[0] + moved[1] + moved[2])
            totals.append(moved[3] + moved[4] + moved[5])
        best = functools.reduce(jnp.maximum, tops)
        factors = [jnp.exp2((top - best) * SCALE) for top in tops]
        whole = sum(factor * total for factor, total in zip(factors, totals))
        shares = [factor / whole for factor in factors]
        for group in range(GROUPS):
            first = head * WIDE + group * HEAD
            out_ref[0, :, first : first + HEAD] = sum(
                parts[shard][:, first : first + HEAD].astype(jnp.float32)
                * shares[shard][:, group : group + 1]
                for shard in range(shards)
            ).astype(jnp.bfloat16)


def merge(chunk, parts, attended):
    start, heads = chunk
    rows = parts[0].shape[-2]
    operands, specs, aliases = list(parts), [VMEM] * len(parts), {}
    if attended is not None:
        operands.append(attended)
        specs.append(HBM)
        aliases = {len(operands) - 1: 0}
    return pl.pallas_call(
        functools.partial(merge_kernel, heads, len(parts)),
        grid=(1,),
        out_shape=jax.ShapeDtypeStruct((1, rows, QHEADS * HEAD), jnp.bfloat16),
        in_specs=specs,
        out_specs=pl.BlockSpec((1, rows, heads * WIDE), lambda i: (0, 0, start // heads)),
        input_output_aliases=aliases,
        cost_estimate=pl.CostEstimate(
            flops=rows * heads * WIDE * 16, transcendentals=0, bytes_accessed=1 << 20
        ),
        name="merge",
    )(*operands)


def local(
    queries, fresh_kv, cache_pages, stretch_store, stretch_request, recompute_idx, block_mask
):
    shards = lax.axis_size("ctx")
    device = lax.axis_index("ctx")
    stores = lax.axis_size("req")
    pages, page_len = cache_pages.shape[2:4]
    span = pages * page_len
    rows = queries.shape[1]
    tiles = rows // TILE

    order = jnp.arange(stores, dtype=jnp.int32)

    def find(table):
        return jnp.sum(jnp.where(order[:, None] == table[None, :], order[None, :], 0), axis=1, dtype=jnp.int32)

    first, last = CHUNKS
    slots = find(stretch_request[0, 0])
    places = find(stretch_store[0, 0])
    store = cache_pages[0, 0]
    early = lax.all_to_all(
        pack("pack", first, slots, store), "req", split_axis=0, concat_axis=0, tiled=True
    )
    late = lax.all_to_all(
        pack("pack_rest", last, slots, store), "req", split_axis=0, concat_axis=0, tiled=True
    )

    own_idx = lax.dynamic_index_in_dim(recompute_idx[0], device, 0, keepdims=False)
    own_pos = device * span + own_idx
    rotated = rotary(queries[0], own_pos, QHEADS).astype(jnp.bfloat16)
    twin = lax.ppermute(rotated, "ctx", [(i, i ^ 1) for i in range(shards)])
    pair = jnp.stack([rotated, twin])
    query = jnp.concatenate(
        [pair]
        + [
            lax.ppermute(pair, "ctx", [(i, (i + 2 * s) % shards) for i in range(shards)])
            for s in range(1, shards // 2)
        ]
    )

    def slot_of(shard):
        odd = (shard ^ device) & 1
        return (device - (shard ^ odd)) % shards + odd

    fresh_rows = fresh_kv[0]
    fresh = jnp.concatenate(
        [rotary(fresh_rows[:, :FEATURE], own_pos, KVHEADS), fresh_rows[:, FEATURE:].astype(jnp.float32)],
        axis=1,
    ).astype(jnp.bfloat16)

    mask_cols = lax.dynamic_index_in_dim(block_mask[0], device, 2, keepdims=False) == 1
    shard_ids = jnp.arange(shards, dtype=jnp.int32)
    far = (mask_cols & (shard_ids > device)[:, None, None]).reshape(shards * tiles, pages)
    own_mask = lax.dynamic_index_in_dim(mask_cols, device, 0, keepdims=False)
    page_ids = jnp.arange(pages, dtype=jnp.int32)
    near = jnp.repeat(own_mask, TILE, axis=0) | (page_ids[None, :] == (own_idx // page_len)[:, None])
    spare = LANES - shards * tiles - rows
    allowed = jnp.concatenate([far, near, jnp.ones((spare, pages), bool)], axis=0).T
    limit = jnp.concatenate(
        [
            jnp.full((shards * tiles,), span, jnp.int32),
            own_idx,
            jnp.full((spare,), span, jnp.int32),
        ]
    )
    key_ids = jnp.arange(span, dtype=jnp.int32).reshape(pages, page_len)
    bias = jnp.where(
        allowed[:, None, :] & (key_ids[:, :, None] <= limit[None, None, :]), 0.0, NEG
    ).astype(jnp.bfloat16).reshape(span, LANES)
    row_ids = jnp.arange(rows, dtype=jnp.int32)
    column = jnp.where(
        (shard_ids == device)[:, None],
        shards * tiles + row_ids[None, :],
        shard_ids[:, None] * tiles + row_ids[None, :] // TILE,
    )
    pick = (column[:, :, None] == jnp.arange(LANES, dtype=jnp.int32)).astype(jnp.bfloat16)

    turn = (device + shard_ids) % shards
    joined, *parts = attend(
        first, shards, (places, turn, slot_of(turn), own_idx), early, fresh, query, pick, bias, None
    )
    parts = [parts[0]] + [
        lax.ppermute(parts[s], "ctx", [(i, (i + s) % shards) for i in range(shards)])
        for s in range(1, shards)
    ]
    attended = merge(first, parts, None)
    joined, part = attend(
        last, 1, (places, shard_ids, slot_of(shard_ids), own_idx), late, fresh, query, pick, bias, joined, [attended]
    )
    part = lax.all_to_all(part, "ctx", split_axis=0, concat_axis=0, tiled=True)
    attended = merge(last, [part], attended)
    return attended, joined


def solution(mesh):
    return jax.shard_map(
        local,
        mesh=mesh,
        in_specs=(
            P("req", "ctx", None),
            P("req", "ctx", None),
            P("req", "ctx", None, None, None),
            P("req", "ctx", None),
            P("req", "ctx", None),
            P("req", None, None),
            P("req", None, None, None, None),
        ),
        out_specs=(P("req", "ctx", None), P("req", "ctx", None)),
        check_vma=False,
    )
```

time: 177 us -> 155 us (0.88)
  waiting for transfers between devices: 81.1 us -> 48.2 us
  blocking collectives: 0 us -> 18.9 us
  between operations: 14.3 us -> 0.93 us
  starting transfers between devices: 25.7 us -> 38 us
  local copies, waits for them, and re-layouts: 11.6 us -> 5.39 us
  Pallas kernels: 39.3 us -> 34.3 us
  other arithmetic: 3.79 us -> 8.19 us
    all_to_all x4 -> x2, waiting for transfers between devices: 81.1 us -> 44 us  [the longest x1 31.4 us: local(): lax.all_to_all(pack('pack', first, slots, store), 'req', split_axis=0, co...]
    ppermute x0 -> x11, starting transfers between devices: none -> 23.6 us  [the longest x7 16 us: local(): lax.ppermute(parts[s], 'ctx', [(i, (i + s) % shards) for i in range(shard...]
    all_to_all x0 -> x1, blocking collectives: none -> 18.9 us  [local(): part = lax.all_to_all(part, 'ctx', split_axis=0, concat_axis=0, tiled=True)]
    all_to_all x4 -> x2, starting transfers between devices: 25.7 us -> 14.4 us  [the longest x1 9.89 us: local(): lax.all_to_all(pack('pack', first, slots, store), 'req', split_axis=0, co...]
    unnamed x25 -> x32, local copies, waits for them, and re-layouts: 10.4 us -> 3.54 us
    pallas_call x5 -> x6, Pallas kernels: 39.3 us -> 34.3 us  [the longest x2 22.1 us: attend(): pl.pallas_call(functools.partial(attend_kernel, start, heads, len(operand...]
    ppermute x0 -> x11, waiting for transfers between devices: none -> 4.17 us  [the longest x7 4.16 us: local(): lax.ppermute(parts[s], 'ctx', [(i, (i + s) % shards) for i in range(shard...]
  transfers between devices with their start and end apart: 5 -> 13, of which waited for: 4 -> 4; matrix products, arithmetic and copies ran while one was open for 2% -> 7% of each run, Pallas kernels for 20% -> 11%
where the time goes in v2:
time: 155 us; the launch traced here: 154 us
  waiting for transfers between devices  48.2 us (31%)
  starting transfers between devices  38 us (25%)
  Pallas kernels  34.3 us (22%)
  blocking collectives  18.9 us (12%)
  other arithmetic  8.19 us (5%)
  local copies, waits for them, and re-layouts  5.39 us (3%)
    all_to_all x1, waiting for transfers between devices, local(): lax.all_to_all(pack('pack', first, slots, store), 'req', split_axis=0, co...  31.4 us
    pallas_call x2, Pallas kernels, attend(): pl.pallas_call(functools.partial(attend_kernel, start, heads, len(operand...  22.1 us
    all_to_all x1, blocking collectives, local(): part = lax.all_to_all(part, 'ctx', split_axis=0, concat_axis=0, tiled=True)  18.9 us
    ppermute x7, starting transfers between devices, local(): lax.ppermute(parts[s], 'ctx', [(i, (i + s) % shards) for i in range(shard...  16 us
    all_to_all x1, waiting for transfers between devices, local(): lax.all_to_all(pack('pack_rest', last, slots, store), 'req', split_axis=0...  12.6 us
    all_to_all x1, starting transfers between devices, local(): lax.all_to_all(pack('pack', first, slots, store), 'req', split_axis=0, co...  9.89 us
    pallas_call x2, Pallas kernels, pack(): pl.pallas_call(functools.partial(pack_kernel, chunk), out_shape=jax.Shape...  7.37 us
    pallas_call x2, Pallas kernels, merge(): pl.pallas_call(functools.partial(merge_kernel, heads, len(parts)), grid=(...  4.9 us
  transfers between devices with their start and end apart: 13, of which 4 were waited for; matrix products, arithmetic and copies ran while one was open for 7% of the time, Pallas kernels for 11%

profile of v2, /device:TPU:32, one launch (start us, length us, event | category | flops | bytes accessed | tf_op | source)
XLA Modules:
  0.0 153.9 jit_solution(5057082896853439212)
XLA Ops:
  0.6 1.3 select_reduce_fusion.slot_ref
  1.9 3.7 %pack.1 = bf16[32,64,512]{2,1,0:T(8,128)(2,1)} custom-call(s32[32]{0:T(128)} %select_reduce_fusion.slot_ref, bf16[32,64,1024]{2,1,0:T(8,128)(2,1)} %bitcast.32), custom_call_target="tpu_custom_call" | custom-call | bytes 8388608 | tf_op jit(solution)/shard_map/pack/pallas_call | solution.py:77
  5.6 9.9 %all-to-all-start.1 = ((bf16[32,64,512]{2,1,0:T(8,128)(2,1)}), bf16[32,64,512]{2,1,0:T(8,128)(2,1)S(1)}, u32[]{:S(2)}, u32[]{:S(2)}) async-start(bf16[32,64,512]{2,1,0:T(8,128)(2,1)} %pack.1), calls=%async_computation.1 | async-start | bytes 4194304 | tf_op jit(solution)/shard_map/all_to_all | solution.py:353
  15.6 0.7 and_select_fusion.2
  16.4 0.1 multiply_cosine_fusion
  16.5 0.1 multiply_subtract_fusion
  16.6 0.1 maximum_convert_fusion
  16.8 3.0 %collective-permute-start = (bf16[16,4096]{1,0:T(8,128)(2,1)S(1)}, bf16[16,4096]{1,0:T(8,128)(2,1)S(1)}, u32[]{:S(2)}, u32[]{:S(2)}) collective-permute-start(bf16[16,4096]{1,0:T(8,128)(2,1)S(1)} %bitcast.37), channel_id=1, source_target_pairs={{0,1},{1,0},{2,3},{3,2},{4,5},{5,4},{6,7},{7,6},{8,9},{9,8},{10,11... | collective-permute-start | bytes 393224 | tf_op jit(solution)/shard_map/ppermute | solution.py:363
  19.9 0.1 and.76
  20.0 0.9 fusion.8
  21.1 0.1 copy.16
  21.2 0.1 copy.15
  21.5 0.6 and_select_fusion.1
  22.1 0.6 select_reduce_fusion.1.place_ref
  22.7 0.1 subtract_convert_fusion
  22.8 0.1 pad_maximum_fusion.2
  23.0 0.7 fusion.pick_ref
  23.7 0.7 constant_dynamic-update-slice_fusion.4
  24.5 3.7 %pack_rest.1 = bf16[32,64,512]{2,1,0:T(8,128)(2,1)} custom-call(s32[32]{0:T(128)} %select_reduce_fusion.slot_ref, bf16[32,64,1024]{2,1,0:T(8,128)(2,1)} %bitcast.33), custom_call_target="tpu_custom_call" | custom-call | bytes 8388608 | tf_op jit(solution)/shard_map/pack_rest/pallas_call | solution.py:77
  28.3 1.1 select_convert_fusion.bias_ref
  29.4 0.6 pad_maximum_fusion.1.fresh_ref
  30.1 2.8 %collective-permute-start.3 = (bf16[2,16,4096]{2,1,0:T(8,128)(2,1)S(1)}, bf16[2,16,4096]{2,1,0:T(8,128)(2,1)S(1)}, u32[]{:S(2)}, u32[]{:S(2)}) collective-permute-start(bf16[2,16,4096]{2,1,0:T(8,128)(2,1)S(1)} %pad_maximum_fusion), channel_id=1, source_target_pairs={{0,6},{1,7},{2,0},{3,1},{4,2},{5,3},{6,4},{7,5},{8,14},{9,15},{10,... | collective-permute-start | bytes 786440 | tf_op jit(solution)/shard_map/ppermute | solution.py:368
  32.9 0.8 collective-permute-start.2
  33.7 0.9 collective-permute-start.1
  34.6 31.4 %all-to-all-done.1.refs_0_ = bf16[32,64,512]{2,1,0:T(8,128)(2,1)S(1)} async-done(((bf16[32,64,512]{2,1,0:T(8,128)(2,1)}), bf16[32,64,512]{2,1,0:T(8,128)(2,1)S(1)}, u32[]{:S(2)}, u32[]{:S(2)}) %all-to-all-start.1) | async-done | bytes 2097184 | tf_op jit(solution)/shard_map/all_to_all | solution.py:353
  66.0 4.5 %all-to-all-start = ((bf16[32,64,512]{2,1,0:T(8,128)(2,1)}), bf16[32,64,512]{2,1,0:T(8,128)(2,1)}, u32[]{:S(2)}, u32[]{:S(2)}) async-start(bf16[32,64,512]{2,1,0:T(8,128)(2,1)} %pack_rest.1), calls=%async_computation | async-start | bytes 4194304 | tf_op jit(solution)/shard_map/all_to_all | solution.py:356
  70.6 0.7 constant_dynamic-update-slice_fusion.3
  71.2 0.7 constant_dynamic-update-slice_fusion.2
  72.0 0.7 constant_dynamic-update-slice_fusion.1
  72.7 0.7 constant_dynamic-update-slice_fusion.query_ref
  73.4 11.1 %attend.2 = (bf16[1,2048,1024]{2,1,0:T(8,128)(2,1)}, bf16[16,2304]{1,0:T(8,128)(2,1)}, bf16[16,2304]{1,0:T(8,128)(2,1)}, bf16[16,2304]{1,0:T(8,128)(2,1)}, bf16[...) custom-call(s32[32]{0:T(128)} %select_reduce_fusion.1.place_ref, ...), custom_call_target="tpu_custom_call" | custom-call | flops 21474836480 | bytes 4194304 | tf_op jit(solution)/shard_map/attend/pallas_call | solution.py:257
  84.5 3.0 %collective-permute-start.4 = (bf16[16,2304]{1,0:T(8,128)(2,1)}, bf16[16,2304]{1,0:T(8,128)(2,1)S(1)}, u32[]{:S(2)}, u32[]{:S(2)}) collective-permute-start(bf16[16,2304]{1,0:T(8,128)(2,1)} %get-tuple-element.15), channel_id=1, source_target_pairs={{0,1},{1,2},{2,3},{3,4},{4,5},{5,6},{6,7},{7,0},{8,9},{9,10},{10,1... | collective-permute-start | bytes 221192 | tf_op jit(solution)/shard_map/ppermute | solution.py:415
  87.5 1.5 collective-permute-start.5
  89.0 2.2 %collective-permute-start.6 = (bf16[16,2304]{1,0:T(8,128)(2,1)}, bf16[16,2304]{1,0:T(8,128)(2,1)S(1)}, u32[]{:S(2)}, u32[]{:S(2)}) collective-permute-start(bf16[16,2304]{1,0:T(8,128)(2,1)} %get-tuple-element.17), channel_id=1, source_target_pairs={{0,3},{1,4},{2,5},{3,6},{4,7},{5,0},{6,1},{7,2},{8,11},{9,12},{10,... | collective-permute-start | bytes 221192 | tf_op jit(solution)/shard_map/ppermute | solution.py:415
  91.2 2.0 %collective-permute-start.7 = (bf16[16,2304]{1,0:T(8,128)(2,1)}, bf16[16,2304]{1,0:T(8,128)(2,1)S(1)}, u32[]{:S(2)}, u32[]{:S(2)}) collective-permute-start(bf16[16,2304]{1,0:T(8,128)(2,1)} %get-tuple-element.18), channel_id=1, source_target_pairs={{0,4},{1,5},{2,6},{3,7},{4,0},{5,1},{6,2},{7,3},{8,12},{9,13},{10,... | collective-permute-start | bytes 221192 | tf_op jit(solution)/shard_map/ppermute | solution.py:415
  93.2 4.5 %collective-permute-start.8 = (bf16[16,2304]{1,0:T(8,128)(2,1)}, bf16[16,2304]{1,0:T(8,128)(2,1)S(1)}, u32[]{:S(2)}, u32[]{:S(2)}) collective-permute-start(bf16[16,2304]{1,0:T(8,128)(2,1)} %get-tuple-element.19), channel_id=1, source_target_pairs={{0,5},{1,6},{2,7},{3,0},{4,1},{5,2},{6,3},{7,4},{8,13},{9,14},{10,... | collective-permute-start | bytes 221192 | tf_op jit(solution)/shard_map/ppermute | solution.py:415
  97.7 1.4 collective-permute-start.9
  99.1 1.5 collective-permute-start.10
  100.6 0.6 fusion.2.from_ref
  101.2 1.8 %collective-permute-done.9.refs_6_ = bf16[16,2304]{1,0:T(8,128)(2,1)S(1)} collective-permute-done((bf16[16,2304]{1,0:T(8,128)(2,1)}, bf16[16,2304]{1,0:T(8,128)(2,1)S(1)}, u32[]{:S(2)}, u32[]{:S(2)}) %collective-permute-start.9) | collective-permute-done | bytes 73760 | tf_op jit(solution)/shard_map/ppermute | solution.py:415
  103.0 2.4 %collective-permute-done.10.refs_7_ = bf16[16,2304]{1,0:T(8,128)(2,1)S(1)} collective-permute-done((bf16[16,2304]{1,0:T(8,128)(2,1)}, bf16[16,2304]{1,0:T(8,128)(2,1)S(1)}, u32[]{:S(2)}, u32[]{:S(2)}) %collective-permute-start.10) | collective-permute-done | bytes 73760 | tf_op jit(solution)/shard_map/ppermute | solution.py:415
  105.4 0.6 copy-done.8
  106.0 2.5 %merge.2.refs_2_.refs_1_ = bf16[1,16,4096]{2,1,0:T(8,128)(2,1)} custom-call(bf16[16,2304]{1,0:T(8,128)(2,1)} %get-tuple-element.14.refs_0_, bf16[16,2304]{1,0:T(8,128)(2,1)} %copy-done.2, bf16[16,2304]{1,0:T(8,128)(2,1)} %copy-done.3, bf16[16,2304]{1,0:T(8,128)(2,1)} %copy-done.4, bf16[16,2304]{1,0:T(8,128)(2,1)} %copy-done.5, bf16[16,2304]{1,0:T(8,128)(2,1)} %copy-done.6, ...), custom_call_target="tpu_custom_call" | custom-call | flops 524288 | bytes 1048576 | tf_op jit(solution)/shard_map/merge/pallas_call | solution.py:319
  108.5 12.6 %all-to-all-done.refs_0_ = bf16[32,64,512]{2,1,0:T(8,128)(2,1)} async-done(((bf16[32,64,512]{2,1,0:T(8,128)(2,1)}), bf16[32,64,512]{2,1,0:T(8,128)(2,1)}, u32[]{:S(2)}, u32[]{:S(2)}) %all-to-all-start) | async-done | bytes 2097184 | tf_op jit(solution)/shard_map/all_to_all | solution.py:356
  121.1 0.5 iota.59.order_ref
  121.6 10.9 %attend.3 = (bf16[1,2048,1024]{2,1,0:T(8,128)(2,1)}, bf16[8,16,2304]{2,1,0:T(8,128)(2,1)}) custom-call(s32[32]{0:T(128)} %select_reduce_fusion.1.place_ref, s32[8]{0:T(128)} %iota.59.order_ref, s32[8]{0:T(128)} %fusion.2.from_ref, s32[16]{0:T(128)} %copy-done.10, bf16[16,1024]{1,0:T(8,128)(2,1)} %pad_maximum_fusion.1.fresh_ref, ...), custom_call_target="tpu_custom_call", output_to_operand_aliasing={{0}: (9, {})} | custom-call | flops 21474836480 | bytes 4194304 | tf_op jit(solution)/shard_map/attend/pallas_call | solution.py:257
  132.6 18.9 %all_to_all.15.refs_0_ = bf16[8,16,2304]{2,1,0:T(8,128)(2,1)} all-to-all(bf16[8,16,2304]{2,1,0:T(8,128)(2,1)} %get-tuple-element.22), channel_id=1, replica_groups=mesh['req'=32,'ctx'=8] {'ctx'}, dimensions={0} | all-to-all | bytes 1179648 | tf_op jit(solution)/shard_map/all_to_all | solution.py:422
  151.4 2.4 %merge.3 = bf16[1,16,4096]{2,1,0:T(8,128)(2,1)} custom-call(bf16[8,16,2304]{2,1,0:T(8,128)(2,1)} %all_to_all.15.refs_0_, bf16[1,16,4096]{2,1,0:T(8,128)(2,1)} %merge.2.refs_2_.refs_1_), custom_call_target="tpu_custom_call", output_to_operand_aliasing={{}: (1, {})} | custom-call | flops 524288 | bytes 1048576 | tf_op jit(solution)/shard_map/merge/pallas_call | solution.py:319
  (60 shorter events, 1.0 us)
Async XLA Ops:
  5.6 10.0 %copy-start.1 = (bf16[1,16,4096]{2,1,0:T(8,128)(2,1)S(1)}, bf16[1,16,4096]{2,1,0:T(8,128)(2,1)}, u32[]{:S(2)}) copy-start(bf16[1,16,4096]{2,1,0:T(8,128)(2,1)} %param.7) | copy-start | bytes 393220
  5.6 60.4 %all-to-all-start.1 = ((bf16[32,64,512]{2,1,0:T(8,128)(2,1)}), bf16[32,64,512]{2,1,0:T(8,128)(2,1)S(1)}, u32[]{:S(2)}, u32[]{:S(2)}) async-start(bf16[32,64,512]{2,1,0:T(8,128)(2,1)} %pack.1), calls=%async_computation.1 | async-start | bytes 4194304 | tf_op jit(solution)/shard_map/all_to_all | solution.py:353
  15.5 5.8 %copy-start.9 = (bf16[1,16,1024]{2,1,0:T(8,128)(2,1)S(1)}, bf16[1,16,1024]{2,1,0:T(8,128)(2,1)}, u32[]{:S(2)}) copy-start(bf16[1,16,1024]{2,1,0:T(8,128)(2,1)} %param.8) | copy-start | bytes 98308
  15.5 6.6 %copy-start.11 = (s32[1,1,32]{2,1,0:T(1,128)S(1)}, s32[1,1,32]{2,1,0:T(1,128)}, u32[]{:S(2)}) copy-start(s32[1,1,32]{2,1,0:T(1,128)} %param.10) | copy-start | bytes 388
  16.3 11.9 %copy-start.10 = (s32[16]{0:T(128)}, s32[16]{0:T(128)S(1)}, u32[]{:S(2)}) copy-start(s32[16]{0:T(128)S(1)} %get-tuple-element.27.idx_ref) | copy-start | bytes 196
  16.8 13.2 %collective-permute-start = (bf16[16,4096]{1,0:T(8,128)(2,1)S(1)}, bf16[16,4096]{1,0:T(8,128)(2,1)S(1)}, u32[]{:S(2)}, u32[]{:S(2)}) collective-permute-start(bf16[16,4096]{1,0:T(8,128)(2,1)S(1)} %bitcast.37), channel_id=1, source_target_pairs={{0,1},{1,0},{2,3},{3,2},{4,5},{5,4},{6,7},{7,6},{8,9},{9,8},{10,11... | collective-permute-start | bytes 393224 | tf_op jit(solution)/shard_map/ppermute | solution.py:363
  30.1 42.6 %collective-permute-start.3 = (bf16[2,16,4096]{2,1,0:T(8,128)(2,1)S(1)}, bf16[2,16,4096]{2,1,0:T(8,128)(2,1)S(1)}, u32[]{:S(2)}, u32[]{:S(2)}) collective-permute-start(bf16[2,16,4096]{2,1,0:T(8,128)(2,1)S(1)} %pad_maximum_fusion), channel_id=1, source_target_pairs={{0,6},{1,7},{2,0},{3,1},{4,2},{5,3},{6,4},{7,5},{8,14},{9,15},{10,... | collective-permute-start | bytes 786440 | tf_op jit(solution)/shard_map/ppermute | solution.py:368
  32.9 39.1 %collective-permute-start.2 = (bf16[2,16,4096]{2,1,0:T(8,128)(2,1)S(1)}, bf16[2,16,4096]{2,1,0:T(8,128)(2,1)S(1)}, u32[]{:S(2)}, u32[]{:S(2)}) collective-permute-start(bf16[2,16,4096]{2,1,0:T(8,128)(2,1)S(1)} %pad_maximum_fusion), channel_id=1, source_target_pairs={{0,4},{1,5},{2,6},{3,7},{4,0},{5,1},{6,2},{7,3},{8,12},{9,13},{10,... | collective-permute-start | bytes 786440 | tf_op jit(solution)/shard_map/ppermute | solution.py:368
  33.7 37.5 %collective-permute-start.1 = (bf16[2,16,4096]{2,1,0:T(8,128)(2,1)S(1)}, bf16[2,16,4096]{2,1,0:T(8,128)(2,1)S(1)}, u32[]{:S(2)}, u32[]{:S(2)}) collective-permute-start(bf16[2,16,4096]{2,1,0:T(8,128)(2,1)S(1)} %pad_maximum_fusion), channel_id=1, source_target_pairs={{0,2},{1,3},{2,4},{3,5},{4,6},{5,7},{6,0},{7,1},{8,10},{9,11},{10,... | collective-permute-start | bytes 786440 | tf_op jit(solution)/shard_map/ppermute | solution.py:368
  66.0 5.2 %copy-start = (bf16[32,64,512]{2,1,0:T(8,128)(2,1)}, bf16[32,64,512]{2,1,0:T(8,128)(2,1)S(1)}, u32[]{:S(2)}) copy-start(bf16[32,64,512]{2,1,0:T(8,128)(2,1)S(1)} %all-to-all-done.1.refs_0_) | copy-start | bytes 6291460
  66.0 55.1 %all-to-all-start = ((bf16[32,64,512]{2,1,0:T(8,128)(2,1)}), bf16[32,64,512]{2,1,0:T(8,128)(2,1)}, u32[]{:S(2)}, u32[]{:S(2)}) async-start(bf16[32,64,512]{2,1,0:T(8,128)(2,1)} %pack_rest.1), calls=%async_computation | async-start | bytes 4194304 | tf_op jit(solution)/shard_map/all_to_all | solution.py:356
  84.5 13.1 %collective-permute-start.4 = (bf16[16,2304]{1,0:T(8,128)(2,1)}, bf16[16,2304]{1,0:T(8,128)(2,1)S(1)}, u32[]{:S(2)}, u32[]{:S(2)}) collective-permute-start(bf16[16,2304]{1,0:T(8,128)(2,1)} %get-tuple-element.15), channel_id=1, source_target_pairs={{0,1},{1,2},{2,3},{3,4},{4,5},{5,6},{6,7},{7,0},{8,9},{9,10},{10,1... | collective-permute-start | bytes 221192 | tf_op jit(solution)/shard_map/ppermute | solution.py:415
  87.5 11.6 %collective-permute-start.5 = (bf16[16,2304]{1,0:T(8,128)(2,1)}, bf16[16,2304]{1,0:T(8,128)(2,1)S(1)}, u32[]{:S(2)}, u32[]{:S(2)}) collective-permute-start(bf16[16,2304]{1,0:T(8,128)(2,1)} %get-tuple-element.16), channel_id=1, source_target_pairs={{0,2},{1,3},{2,4},{3,5},{4,6},{5,7},{6,0},{7,1},{8,10},{9,11},{10,... | collective-permute-start | bytes 221192 | tf_op jit(solution)/shard_map/ppermute | solution.py:415
  89.0 12.2 %collective-permute-start.6 = (bf16[16,2304]{1,0:T(8,128)(2,1)}, bf16[16,2304]{1,0:T(8,128)(2,1)S(1)}, u32[]{:S(2)}, u32[]{:S(2)}) collective-permute-start(bf16[16,2304]{1,0:T(8,128)(2,1)} %get-tuple-element.17), channel_id=1, source_target_pairs={{0,3},{1,4},{2,5},{3,6},{4,7},{5,0},{6,1},{7,2},{8,11},{9,12},{10,... | collective-permute-start | bytes 221192 | tf_op jit(solution)/shard_map/ppermute | solution.py:415
  91.2 10.0 %collective-permute-start.7 = (bf16[16,2304]{1,0:T(8,128)(2,1)}, bf16[16,2304]{1,0:T(8,128)(2,1)S(1)}, u32[]{:S(2)}, u32[]{:S(2)}) collective-permute-start(bf16[16,2304]{1,0:T(8,128)(2,1)} %get-tuple-element.18), channel_id=1, source_target_pairs={{0,4},{1,5},{2,6},{3,7},{4,0},{5,1},{6,2},{7,3},{8,12},{9,13},{10,... | collective-permute-start | bytes 221192 | tf_op jit(solution)/shard_map/ppermute | solution.py:415
  93.2 8.0 %collective-permute-start.8 = (bf16[16,2304]{1,0:T(8,128)(2,1)}, bf16[16,2304]{1,0:T(8,128)(2,1)S(1)}, u32[]{:S(2)}, u32[]{:S(2)}) collective-permute-start(bf16[16,2304]{1,0:T(8,128)(2,1)} %get-tuple-element.19), channel_id=1, source_target_pairs={{0,5},{1,6},{2,7},{3,0},{4,1},{5,2},{6,3},{7,4},{8,13},{9,14},{10,... | collective-permute-start | bytes 221192 | tf_op jit(solution)/shard_map/ppermute | solution.py:415
  97.7 7.7 %copy-start.2 = (bf16[16,2304]{1,0:T(8,128)(2,1)}, bf16[16,2304]{1,0:T(8,128)(2,1)S(1)}, u32[]{:S(2)}) copy-start(bf16[16,2304]{1,0:T(8,128)(2,1)S(1)} %collective-permute-done.4.refs_1_) | copy-start | bytes 221188
  97.7 5.3 %collective-permute-start.9 = (bf16[16,2304]{1,0:T(8,128)(2,1)}, bf16[16,2304]{1,0:T(8,128)(2,1)S(1)}, u32[]{:S(2)}, u32[]{:S(2)}) collective-permute-start(bf16[16,2304]{1,0:T(8,128)(2,1)} %get-tuple-element.20), channel_id=1, source_target_pairs={{0,6},{1,7},{2,0},{3,1},{4,2},{5,3},{6,4},{7,5},{8,14},{9,15},{10,... | collective-permute-start | bytes 221192 | tf_op jit(solution)/shard_map/ppermute | solution.py:415
  99.1 6.3 %copy-start.3 = (bf16[16,2304]{1,0:T(8,128)(2,1)}, bf16[16,2304]{1,0:T(8,128)(2,1)S(1)}, u32[]{:S(2)}) copy-start(bf16[16,2304]{1,0:T(8,128)(2,1)S(1)} %collective-permute-done.5.refs_2_) | copy-start | bytes 221188
  99.1 6.3 %collective-permute-start.10 = (bf16[16,2304]{1,0:T(8,128)(2,1)}, bf16[16,2304]{1,0:T(8,128)(2,1)S(1)}, u32[]{:S(2)}, u32[]{:S(2)}) collective-permute-start(bf16[16,2304]{1,0:T(8,128)(2,1)} %get-tuple-element.21), channel_id=1, source_target_pairs={{0,7},{1,0},{2,1},{3,2},{4,3},{5,4},{6,5},{7,6},{8,15},{9,8},{10,9... | collective-permute-start | bytes 221192 | tf_op jit(solution)/shard_map/ppermute | solution.py:415
  101.2 4.2 %copy-start.4 = (bf16[16,2304]{1,0:T(8,128)(2,1)}, bf16[16,2304]{1,0:T(8,128)(2,1)S(1)}, u32[]{:S(2)}) copy-start(bf16[16,2304]{1,0:T(8,128)(2,1)S(1)} %collective-permute-done.6.refs_3_) | copy-start | bytes 221188
  101.2 4.2 %copy-start.5 = (bf16[16,2304]{1,0:T(8,128)(2,1)}, bf16[16,2304]{1,0:T(8,128)(2,1)S(1)}, u32[]{:S(2)}) copy-start(bf16[16,2304]{1,0:T(8,128)(2,1)S(1)} %collective-permute-done.7.refs_4_) | copy-start | bytes 221188
  101.2 4.2 %copy-start.6 = (bf16[16,2304]{1,0:T(8,128)(2,1)}, bf16[16,2304]{1,0:T(8,128)(2,1)S(1)}, u32[]{:S(2)}) copy-start(bf16[16,2304]{1,0:T(8,128)(2,1)S(1)} %collective-permute-done.8.refs_5_) | copy-start | bytes 221188
  103.0 2.4 %copy-start.7 = (bf16[16,2304]{1,0:T(8,128)(2,1)}, bf16[16,2304]{1,0:T(8,128)(2,1)S(1)}, u32[]{:S(2)}) copy-start(bf16[16,2304]{1,0:T(8,128)(2,1)S(1)} %collective-permute-done.9.refs_6_) | copy-start | bytes 221188
  105.4 0.6 copy-start.8

commit v3 on v2

--- a/solution.py
+++ b/solution.py
@@ -50,28 +50,28 @@
     return ((start * HEAD, width, 0), (FEATURE + start * HEAD, width, width))
 
 
-def pack_kernel(chunk, slot_ref, pages_ref, out_ref, held, in_sem, out_sem):
+def pack_kernel(chunk, owner_ref, pages_ref, out_ref, held, in_sem, out_sem):
     loads, saves = [], []
-    for owner in range(pages_ref.shape[0]):
+    for slot in range(pages_ref.shape[0]):
         for half, (start, width, column) in enumerate(ways(chunk)):
             load = pltpu.make_async_copy(
-                pages_ref.at[slot_ref[owner], :, pl.ds(start, width)],
-                held.at[owner, :, pl.ds(column, width)],
-                in_sem.at[owner, half],
+                pages_ref.at[slot, :, pl.ds(start, width)],
+                held.at[slot, :, pl.ds(column, width)],
+                in_sem.at[slot, half],
             )
             load.start()
             loads.append(load)
-    for owner in range(pages_ref.shape[0]):
-        loads[2 * owner].wait()
-        loads[2 * owner + 1].wait()
-        save = pltpu.make_async_copy(held.at[owner], out_ref.at[owner], out_sem.at[owner])
+    for slot in range(pages_ref.shape[0]):
+        loads[2 * slot].wait()
+        loads[2 * slot + 1].wait()
+        save = pltpu.make_async_copy(held.at[slot], out_ref.at[owner_ref[slot]], out_sem.at[slot])
         save.start()
         saves.append(save)
     for save in saves:
         save.wait()
 
 
-def pack(name, chunk, slots, pages):
+def pack(name, chunk, owners, pages):
     count, page_len, _ = pages.shape
     shape = (count, page_len, 2 * chunk[1] * HEAD)
     return pl.pallas_call(
@@ -87,7 +87,7 @@
         compiler_params=pltpu.CompilerParams(vmem_limit_bytes=60 << 20),
         cost_estimate=pl.CostEstimate(flops=0, transcendentals=0, bytes_accessed=8 << 20),
         name=name,
-    )(slots, pages)
+    )(owners, pages)
 
 
 BLOCK = 2
@@ -95,7 +95,7 @@
 
 
 def attend_kernel(
-    start, heads, held_back, count, place_ref, order_ref, from_ref, idx_ref, fresh_ref,
+    start, heads, held_back, count, store_ref, order_ref, from_ref, idx_ref, fresh_ref,
     query_ref, pick_ref, bias_ref, *refs,
 ):
     arrived_ref, refs = refs[0], refs[held_back:]
@@ -110,9 +110,9 @@
     if count == 1:
         parts = [parts[0].at[shard] for shard in range(shards)]
 
-    for source in range(pages):
-        place = pl.ds(pl.multiple_of(place_ref[source] * page_len, page_len), page_len)
-        pltpu.make_async_copy(arrived_ref.at[source], held.at[place], load_sem).start()
+    for page in range(pages):
+        place = pl.ds(page * page_len, page_len)
+        pltpu.make_async_copy(arrived_ref.at[store_ref[page]], held.at[place], load_sem).start()
     keys[:, HEAD:] = bias_ref[...]
     pltpu.make_async_copy(held, held, load_sem).wait()
 
@@ -335,26 +335,20 @@
 ):
     shards = lax.axis_size("ctx")
     device = lax.axis_index("ctx")
-    stores = lax.axis_size("req")
     pages, page_len = cache_pages.shape[2:4]
     span = pages * page_len
     rows = queries.shape[1]
     tiles = rows // TILE
 
-    order = jnp.arange(stores, dtype=jnp.int32)
-
-    def find(table):
-        return jnp.sum(jnp.where(order[:, None] == table[None, :], order[None, :], 0), axis=1, dtype=jnp.int32)
-
     first, last = CHUNKS
-    slots = find(stretch_request[0, 0])
-    places = find(stretch_store[0, 0])
+    owners = stretch_request[0, 0]
+    places = stretch_store[0, 0]
     store = cache_pages[0, 0]
     early = lax.all_to_all(
-        pack("pack", first, slots, store), "req", split_axis=0, concat_axis=0, tiled=True
+        pack("pack", first, owners, store), "req", split_axis=0, concat_axis=0, tiled=True
     )
     late = lax.all_to_all(
-        pack("pack_rest", last, slots, store), "req", split_axis=0, concat_axis=0, tiled=True
+        pack("pack_rest", last, owners, store), "req", split_axis=0, concat_axis=0, tiled=True
     )
 
     own_idx = lax.dynamic_index_in_dim(recompute_idx[0], device, 0, keepdims=False)

time: 155 us -> 154 us (level)
  other arithmetic: 8.19 us -> 6.26 us
    reduce_sum x2 -> x0, other arithmetic: 1.9 us -> none  [find(): jnp.sum(jnp.where(order[:, None] == table[None, :], order[None, :], 0), a...]
    unnamed x32 -> x30, local copies, waits for them, and re-layouts: 3.54 us -> 3.53 us
where the time goes in v3:
time: 154 us; the launch traced here: 153 us
  waiting for transfers between devices  48.7 us (32%)
  starting transfers between devices  38.1 us (25%)
  Pallas kernels  34.3 us (22%)
  blocking collectives  18.9 us (12%)
  other arithmetic  6.26 us (4%)
  local copies, waits for them, and re-layouts  5.37 us (3%)
    all_to_all x1, waiting for transfers between devices, local(): lax.all_to_all(pack('pack', first, owners, store), 'req', split_axis=0, c...  32 us
    pallas_call x2, Pallas kernels, attend(): pl.pallas_call(functools.partial(attend_kernel, start, heads, len(operand...  22.1 us
    all_to_all x1, blocking collectives, local(): part = lax.all_to_all(part, 'ctx', split_axis=0, concat_axis=0, tiled=True)  18.9 us
    ppermute x7, starting transfers between devices, local(): lax.ppermute(parts[s], 'ctx', [(i, (i + s) % shards) for i in range(shard...  16.1 us
    all_to_all x1, waiting for transfers between devices, local(): lax.all_to_all(pack('pack_rest', last, owners, store), 'req', split_axis=...  12.5 us
    all_to_all x1, starting transfers between devices, local(): lax.all_to_all(pack('pack', first, owners, store), 'req', split_axis=0, c...  9.89 us
    pallas_call x2, Pallas kernels, pack(): pl.pallas_call(functools.partial(pack_kernel, chunk), out_shape=jax.Shape...  7.38 us
    pallas_call x2, Pallas kernels, merge(): pl.pallas_call(functools.partial(merge_kernel, heads, len(parts)), grid=(...  4.9 us
  transfers between devices with their start and end apart: 13, of which 4 were waited for; matrix products, arithmetic and copies ran while one was open for 7% of the time, Pallas kernels for 11%

profile of v3, /device:TPU:32, one launch (start us, length us, event | category | flops | bytes accessed | tf_op | source)
XLA Modules:
  0.0 152.6 jit_solution(16296916201884917508)
XLA Ops:
  0.6 3.7 %pack.1 = bf16[32,64,512]{2,1,0:T(8,128)(2,1)} custom-call(s32[32]{0:T(128)} %bitcast.41, bf16[32,64,1024]{2,1,0:T(8,128)(2,1)} %bitcast.32), custom_call_target="tpu_custom_call" | custom-call | bytes 8388608 | tf_op jit(solution)/shard_map/pack/pallas_call | solution.py:77
  4.3 9.9 %all-to-all-start.1 = ((bf16[32,64,512]{2,1,0:T(8,128)(2,1)}), bf16[32,64,512]{2,1,0:T(8,128)(2,1)S(1)}, u32[]{:S(2)}, u32[]{:S(2)}) async-start(bf16[32,64,512]{2,1,0:T(8,128)(2,1)} %pack.1), calls=%async_computation.1 | async-start | bytes 4194304 | tf_op jit(solution)/shard_map/all_to_all | solution.py:347
  14.3 0.7 and_select_fusion.2
  15.0 0.1 multiply_cosine_fusion
  15.2 0.1 multiply_subtract_fusion
  15.3 0.1 maximum_convert_fusion
  15.5 3.0 %collective-permute-start = (bf16[16,4096]{1,0:T(8,128)(2,1)S(1)}, bf16[16,4096]{1,0:T(8,128)(2,1)S(1)}, u32[]{:S(2)}, u32[]{:S(2)}) collective-permute-start(bf16[16,4096]{1,0:T(8,128)(2,1)S(1)} %bitcast.37), channel_id=1, source_target_pairs={{0,1},{1,0},{2,3},{3,2},{4,5},{5,4},{6,7},{7,6},{8,9},{9,8},{10,11... | collective-permute-start | bytes 393224 | tf_op jit(solution)/shard_map/ppermute | solution.py:357
  18.7 0.1 and.76
  18.7 0.9 fusion.8
  19.8 0.1 copy.14
  19.9 0.1 copy.13
  20.2 0.6 and_select_fusion.1
  20.8 0.1 subtract_convert_fusion
  20.9 0.1 pad_maximum_fusion.2
  20.9 0.1 add_bitcast_fusion
  21.1 0.7 fusion.pick_ref
  21.8 0.7 constant_dynamic-update-slice_fusion.4
  22.5 0.1 pad_add_fusion
  22.5 3.7 %pack_rest.1 = bf16[32,64,512]{2,1,0:T(8,128)(2,1)} custom-call(s32[32]{0:T(128)} %bitcast.42, bf16[32,64,1024]{2,1,0:T(8,128)(2,1)} %bitcast.33), custom_call_target="tpu_custom_call" | custom-call | bytes 8388608 | tf_op jit(solution)/shard_map/pack_rest/pallas_call | solution.py:77
  26.4 1.2 select_convert_fusion.bias_ref
  27.5 0.6 pad_maximum_fusion.1.fresh_ref
  28.2 2.8 %collective-permute-start.3 = (bf16[2,16,4096]{2,1,0:T(8,128)(2,1)S(1)}, bf16[2,16,4096]{2,1,0:T(8,128)(2,1)S(1)}, u32[]{:S(2)}, u32[]{:S(2)}) collective-permute-start(bf16[2,16,4096]{2,1,0:T(8,128)(2,1)S(1)} %pad_maximum_fusion), channel_id=1, source_target_pairs={{0,6},{1,7},{2,0},{3,1},{4,2},{5,3},{6,4},{7,5},{8,14},{9,15},{10,... | collective-permute-start | bytes 786440 | tf_op jit(solution)/shard_map/ppermute | solution.py:362
  31.0 0.8 collective-permute-start.2
  31.8 0.9 collective-permute-start.1
  32.7 32.0 %all-to-all-done.1.refs_0_ = bf16[32,64,512]{2,1,0:T(8,128)(2,1)S(1)} async-done(((bf16[32,64,512]{2,1,0:T(8,128)(2,1)}), bf16[32,64,512]{2,1,0:T(8,128)(2,1)S(1)}, u32[]{:S(2)}, u32[]{:S(2)}) %all-to-all-start.1) | async-done | bytes 2097184 | tf_op jit(solution)/shard_map/all_to_all | solution.py:347
  64.7 4.6 %all-to-all-start = ((bf16[32,64,512]{2,1,0:T(8,128)(2,1)}), bf16[32,64,512]{2,1,0:T(8,128)(2,1)}, u32[]{:S(2)}, u32[]{:S(2)}) async-start(bf16[32,64,512]{2,1,0:T(8,128)(2,1)} %pack_rest.1), calls=%async_computation | async-start | bytes 4194304 | tf_op jit(solution)/shard_map/all_to_all | solution.py:350
  69.3 0.7 constant_dynamic-update-slice_fusion.3
  70.0 0.7 constant_dynamic-update-slice_fusion.2
  70.7 0.7 constant_dynamic-update-slice_fusion.1
  71.4 0.7 constant_dynamic-update-slice_fusion.query_ref
  72.1 11.1 %attend.2 = (bf16[1,2048,1024]{2,1,0:T(8,128)(2,1)}, bf16[16,2304]{1,0:T(8,128)(2,1)}, bf16[16,2304]{1,0:T(8,128)(2,1)}, bf16[16,2304]{1,0:T(8,128)(2,1)}, bf16[...) custom-call(s32[32]{0:T(128)} %bitcast.44, ...), custom_call_target="tpu_custom_call" | custom-call | flops 21474836480 | bytes 4194304 | tf_op jit(solution)/shard_map/attend/pallas_call | solution.py:257
  83.3 3.0 %collective-permute-start.4 = (bf16[16,2304]{1,0:T(8,128)(2,1)}, bf16[16,2304]{1,0:T(8,128)(2,1)S(1)}, u32[]{:S(2)}, u32[]{:S(2)}) collective-permute-start(bf16[16,2304]{1,0:T(8,128)(2,1)} %get-tuple-element.15), channel_id=1, source_target_pairs={{0,1},{1,2},{2,3},{3,4},{4,5},{5,6},{6,7},{7,0},{8,9},{9,10},{10,1... | collective-permute-start | bytes 221192 | tf_op jit(solution)/shard_map/ppermute | solution.py:409
  86.2 1.5 collective-permute-start.5
  87.7 2.2 %collective-permute-start.6 = (bf16[16,2304]{1,0:T(8,128)(2,1)}, bf16[16,2304]{1,0:T(8,128)(2,1)S(1)}, u32[]{:S(2)}, u32[]{:S(2)}) collective-permute-start(bf16[16,2304]{1,0:T(8,128)(2,1)} %get-tuple-element.17), channel_id=1, source_target_pairs={{0,3},{1,4},{2,5},{3,6},{4,7},{5,0},{6,1},{7,2},{8,11},{9,12},{10,... | collective-permute-start | bytes 221192 | tf_op jit(solution)/shard_map/ppermute | solution.py:409
  89.9 2.0 %collective-permute-start.7 = (bf16[16,2304]{1,0:T(8,128)(2,1)}, bf16[16,2304]{1,0:T(8,128)(2,1)S(1)}, u32[]{:S(2)}, u32[]{:S(2)}) collective-permute-start(bf16[16,2304]{1,0:T(8,128)(2,1)} %get-tuple-element.18), channel_id=1, source_target_pairs={{0,4},{1,5},{2,6},{3,7},{4,0},{5,1},{6,2},{7,3},{8,12},{9,13},{10,... | collective-permute-start | bytes 221192 | tf_op jit(solution)/shard_map/ppermute | solution.py:409
  91.9 4.5 %collective-permute-start.8 = (bf16[16,2304]{1,0:T(8,128)(2,1)}, bf16[16,2304]{1,0:T(8,128)(2,1)S(1)}, u32[]{:S(2)}, u32[]{:S(2)}) collective-permute-start(bf16[16,2304]{1,0:T(8,128)(2,1)} %get-tuple-element.19), channel_id=1, source_target_pairs={{0,5},{1,6},{2,7},{3,0},{4,1},{5,2},{6,3},{7,4},{8,13},{9,14},{10,... | collective-permute-start | bytes 221192 | tf_op jit(solution)/shard_map/ppermute | solution.py:409
  96.4 1.4 collective-permute-start.9
  97.8 1.5 %collective-permute-start.10 = (bf16[16,2304]{1,0:T(8,128)(2,1)}, bf16[16,2304]{1,0:T(8,128)(2,1)S(1)}, u32[]{:S(2)}, u32[]{:S(2)}) collective-permute-start(bf16[16,2304]{1,0:T(8,128)(2,1)} %get-tuple-element.21), channel_id=1, source_target_pairs={{0,7},{1,0},{2,1},{3,2},{4,3},{5,4},{6,5},{7,6},{8,15},{9,8},{10,9... | collective-permute-start | bytes 221192 | tf_op jit(solution)/shard_map/ppermute | solution.py:409
  99.4 0.6 fusion.2.from_ref
  100.0 1.5 %collective-permute-done.9.refs_6_ = bf16[16,2304]{1,0:T(8,128)(2,1)S(1)} collective-permute-done((bf16[16,2304]{1,0:T(8,128)(2,1)}, bf16[16,2304]{1,0:T(8,128)(2,1)S(1)}, u32[]{:S(2)}, u32[]{:S(2)}) %collective-permute-start.9) | collective-permute-done | bytes 73760 | tf_op jit(solution)/shard_map/ppermute | solution.py:409
  101.5 2.7 %collective-permute-done.10.refs_7_ = bf16[16,2304]{1,0:T(8,128)(2,1)S(1)} collective-permute-done((bf16[16,2304]{1,0:T(8,128)(2,1)}, bf16[16,2304]{1,0:T(8,128)(2,1)S(1)}, u32[]{:S(2)}, u32[]{:S(2)}) %collective-permute-start.10) | collective-permute-done | bytes 73760 | tf_op jit(solution)/shard_map/ppermute | solution.py:409
  104.3 0.6 copy-done.8
  104.8 2.5 %merge.2.refs_2_.refs_1_ = bf16[1,16,4096]{2,1,0:T(8,128)(2,1)} custom-call(bf16[16,2304]{1,0:T(8,128)(2,1)} %get-tuple-element.14.refs_0_, bf16[16,2304]{1,0:T(8,128)(2,1)} %copy-done.2, bf16[16,2304]{1,0:T(8,128)(2,1)} %copy-done.3, bf16[16,2304]{1,0:T(8,128)(2,1)} %copy-done.4, bf16[16,2304]{1,0:T(8,128)(2,1)} %copy-done.5, bf16[16,2304]{1,0:T(8,128)(2,1)} %copy-done.6, ...), custom_call_target="tpu_custom_call" | custom-call | flops 524288 | bytes 1048576 | tf_op jit(solution)/shard_map/merge/pallas_call | solution.py:319
  107.3 12.5 %all-to-all-done.refs_0_ = bf16[32,64,512]{2,1,0:T(8,128)(2,1)} async-done(((bf16[32,64,512]{2,1,0:T(8,128)(2,1)}), bf16[32,64,512]{2,1,0:T(8,128)(2,1)}, u32[]{:S(2)}, u32[]{:S(2)}) %all-to-all-start) | async-done | bytes 2097184 | tf_op jit(solution)/shard_map/all_to_all | solution.py:350
  119.8 0.5 iota.54.order_ref
  120.3 10.9 %attend.3 = (bf16[1,2048,1024]{2,1,0:T(8,128)(2,1)}, bf16[8,16,2304]{2,1,0:T(8,128)(2,1)}) custom-call(s32[32]{0:T(128)} %bitcast.45, s32[8]{0:T(128)} %iota.54.order_ref, s32[8]{0:T(128)} %fusion.2.from_ref, s32[16]{0:T(128)} %copy-done.10, bf16[16,1024]{1,0:T(8,128)(2,1)} %pad_maximum_fusion.1.fresh_ref, ...), custom_call_target="tpu_custom_call", output_to_operand_aliasing={{0}: (9, {})} | custom-call | flops 21474836480 | bytes 4194304 | tf_op jit(solution)/shard_map/attend/pallas_call | solution.py:257
  131.3 18.9 %all_to_all.15.refs_0_ = bf16[8,16,2304]{2,1,0:T(8,128)(2,1)} all-to-all(bf16[8,16,2304]{2,1,0:T(8,128)(2,1)} %get-tuple-element.22), channel_id=1, replica_groups=mesh['req'=32,'ctx'=8] {'ctx'}, dimensions={0} | all-to-all | bytes 1179648 | tf_op jit(solution)/shard_map/all_to_all | solution.py:416
  150.1 2.4 %merge.3 = bf16[1,16,4096]{2,1,0:T(8,128)(2,1)} custom-call(bf16[8,16,2304]{2,1,0:T(8,128)(2,1)} %all_to_all.15.refs_0_, bf16[1,16,4096]{2,1,0:T(8,128)(2,1)} %merge.2.refs_2_.refs_1_), custom_call_target="tpu_custom_call", output_to_operand_aliasing={{}: (1, {})} | custom-call | flops 524288 | bytes 1048576 | tf_op jit(solution)/shard_map/merge/pallas_call | solution.py:319
  (56 shorter events, 0.8 us)
Async XLA Ops:
  4.3 9.9 %copy-start.1 = (bf16[1,16,4096]{2,1,0:T(8,128)(2,1)S(1)}, bf16[1,16,4096]{2,1,0:T(8,128)(2,1)}, u32[]{:S(2)}) copy-start(bf16[1,16,4096]{2,1,0:T(8,128)(2,1)} %param.7) | copy-start | bytes 393220
  4.3 60.4 %all-to-all-start.1 = ((bf16[32,64,512]{2,1,0:T(8,128)(2,1)}), bf16[32,64,512]{2,1,0:T(8,128)(2,1)S(1)}, u32[]{:S(2)}, u32[]{:S(2)}) async-start(bf16[32,64,512]{2,1,0:T(8,128)(2,1)} %pack.1), calls=%async_computation.1 | async-start | bytes 4194304 | tf_op jit(solution)/shard_map/all_to_all | solution.py:347
  14.2 5.8 %copy-start.9 = (bf16[1,16,1024]{2,1,0:T(8,128)(2,1)S(1)}, bf16[1,16,1024]{2,1,0:T(8,128)(2,1)}, u32[]{:S(2)}) copy-start(bf16[1,16,1024]{2,1,0:T(8,128)(2,1)} %param.8) | copy-start | bytes 98308
  15.0 11.3 %copy-start.10 = (s32[16]{0:T(128)}, s32[16]{0:T(128)S(1)}, u32[]{:S(2)}) copy-start(s32[16]{0:T(128)S(1)} %get-tuple-element.27.idx_ref) | copy-start | bytes 196
  15.5 12.6 %collective-permute-start = (bf16[16,4096]{1,0:T(8,128)(2,1)S(1)}, bf16[16,4096]{1,0:T(8,128)(2,1)S(1)}, u32[]{:S(2)}, u32[]{:S(2)}) collective-permute-start(bf16[16,4096]{1,0:T(8,128)(2,1)S(1)} %bitcast.37), channel_id=1, source_target_pairs={{0,1},{1,0},{2,3},{3,2},{4,5},{5,4},{6,7},{7,6},{8,9},{9,8},{10,11... | collective-permute-start | bytes 393224 | tf_op jit(solution)/shard_map/ppermute | solution.py:357
  28.2 43.3 %collective-permute-start.3 = (bf16[2,16,4096]{2,1,0:T(8,128)(2,1)S(1)}, bf16[2,16,4096]{2,1,0:T(8,128)(2,1)S(1)}, u32[]{:S(2)}, u32[]{:S(2)}) collective-permute-start(bf16[2,16,4096]{2,1,0:T(8,128)(2,1)S(1)} %pad_maximum_fusion), channel_id=1, source_target_pairs={{0,6},{1,7},{2,0},{3,1},{4,2},{5,3},{6,4},{7,5},{8,14},{9,15},{10,... | collective-permute-start | bytes 786440 | tf_op jit(solution)/shard_map/ppermute | solution.py:362
  31.0 39.7 %collective-permute-start.2 = (bf16[2,16,4096]{2,1,0:T(8,128)(2,1)S(1)}, bf16[2,16,4096]{2,1,0:T(8,128)(2,1)S(1)}, u32[]{:S(2)}, u32[]{:S(2)}) collective-permute-start(bf16[2,16,4096]{2,1,0:T(8,128)(2,1)S(1)} %pad_maximum_fusion), channel_id=1, source_target_pairs={{0,4},{1,5},{2,6},{3,7},{4,0},{5,1},{6,2},{7,3},{8,12},{9,13},{10,... | collective-permute-start | bytes 786440 | tf_op jit(solution)/shard_map/ppermute | solution.py:362
  31.8 38.2 %collective-permute-start.1 = (bf16[2,16,4096]{2,1,0:T(8,128)(2,1)S(1)}, bf16[2,16,4096]{2,1,0:T(8,128)(2,1)S(1)}, u32[]{:S(2)}, u32[]{:S(2)}) collective-permute-start(bf16[2,16,4096]{2,1,0:T(8,128)(2,1)S(1)} %pad_maximum_fusion), channel_id=1, source_target_pairs={{0,2},{1,3},{2,4},{3,5},{4,6},{5,7},{6,0},{7,1},{8,10},{9,11},{10,... | collective-permute-start | bytes 786440 | tf_op jit(solution)/shard_map/ppermute | solution.py:362
  64.7 5.2 %copy-start = (bf16[32,64,512]{2,1,0:T(8,128)(2,1)}, bf16[32,64,512]{2,1,0:T(8,128)(2,1)S(1)}, u32[]{:S(2)}) copy-start(bf16[32,64,512]{2,1,0:T(8,128)(2,1)S(1)} %all-to-all-done.1.refs_0_) | copy-start | bytes 6291460
  64.7 55.1 %all-to-all-start = ((bf16[32,64,512]{2,1,0:T(8,128)(2,1)}), bf16[32,64,512]{2,1,0:T(8,128)(2,1)}, u32[]{:S(2)}, u32[]{:S(2)}) async-start(bf16[32,64,512]{2,1,0:T(8,128)(2,1)} %pack_rest.1), calls=%async_computation | async-start | bytes 4194304 | tf_op jit(solution)/shard_map/all_to_all | solution.py:350
  83.3 13.1 %collective-permute-start.4 = (bf16[16,2304]{1,0:T(8,128)(2,1)}, bf16[16,2304]{1,0:T(8,128)(2,1)S(1)}, u32[]{:S(2)}, u32[]{:S(2)}) collective-permute-start(bf16[16,2304]{1,0:T(8,128)(2,1)} %get-tuple-element.15), channel_id=1, source_target_pairs={{0,1},{1,2},{2,3},{3,4},{4,5},{5,6},{6,7},{7,0},{8,9},{9,10},{10,1... | collective-permute-start | bytes 221192 | tf_op jit(solution)/shard_map/ppermute | solution.py:409
  86.2 11.6 %collective-permute-start.5 = (bf16[16,2304]{1,0:T(8,128)(2,1)}, bf16[16,2304]{1,0:T(8,128)(2,1)S(1)}, u32[]{:S(2)}, u32[]{:S(2)}) collective-permute-start(bf16[16,2304]{1,0:T(8,128)(2,1)} %get-tuple-element.16), channel_id=1, source_target_pairs={{0,2},{1,3},{2,4},{3,5},{4,6},{5,7},{6,0},{7,1},{8,10},{9,11},{10,... | collective-permute-start | bytes 221192 | tf_op jit(solution)/shard_map/ppermute | solution.py:409
  87.7 12.2 %collective-permute-start.6 = (bf16[16,2304]{1,0:T(8,128)(2,1)}, bf16[16,2304]{1,0:T(8,128)(2,1)S(1)}, u32[]{:S(2)}, u32[]{:S(2)}) collective-permute-start(bf16[16,2304]{1,0:T(8,128)(2,1)} %get-tuple-element.17), channel_id=1, source_target_pairs={{0,3},{1,4},{2,5},{3,6},{4,7},{5,0},{6,1},{7,2},{8,11},{9,12},{10,... | collective-permute-start | bytes 221192 | tf_op jit(solution)/shard_map/ppermute | solution.py:409
  89.9 10.0 %collective-permute-start.7 = (bf16[16,2304]{1,0:T(8,128)(2,1)}, bf16[16,2304]{1,0:T(8,128)(2,1)S(1)}, u32[]{:S(2)}, u32[]{:S(2)}) collective-permute-start(bf16[16,2304]{1,0:T(8,128)(2,1)} %get-tuple-element.18), channel_id=1, source_target_pairs={{0,4},{1,5},{2,6},{3,7},{4,0},{5,1},{6,2},{7,3},{8,12},{9,13},{10,... | collective-permute-start | bytes 221192 | tf_op jit(solution)/shard_map/ppermute | solution.py:409
  91.9 8.0 %collective-permute-start.8 = (bf16[16,2304]{1,0:T(8,128)(2,1)}, bf16[16,2304]{1,0:T(8,128)(2,1)S(1)}, u32[]{:S(2)}, u32[]{:S(2)}) collective-permute-start(bf16[16,2304]{1,0:T(8,128)(2,1)} %get-tuple-element.19), channel_id=1, source_target_pairs={{0,5},{1,6},{2,7},{3,0},{4,1},{5,2},{6,3},{7,4},{8,13},{9,14},{10,... | collective-permute-start | bytes 221192 | tf_op jit(solution)/shard_map/ppermute | solution.py:409
  96.4 7.8 %copy-start.2 = (bf16[16,2304]{1,0:T(8,128)(2,1)}, bf16[16,2304]{1,0:T(8,128)(2,1)S(1)}, u32[]{:S(2)}) copy-start(bf16[16,2304]{1,0:T(8,128)(2,1)S(1)} %collective-permute-done.4.refs_1_) | copy-start | bytes 221188
  96.4 5.1 %collective-permute-start.9 = (bf16[16,2304]{1,0:T(8,128)(2,1)}, bf16[16,2304]{1,0:T(8,128)(2,1)S(1)}, u32[]{:S(2)}, u32[]{:S(2)}) collective-permute-start(bf16[16,2304]{1,0:T(8,128)(2,1)} %get-tuple-element.20), channel_id=1, source_target_pairs={{0,6},{1,7},{2,0},{3,1},{4,2},{5,3},{6,4},{7,5},{8,14},{9,15},{10,... | collective-permute-start | bytes 221192 | tf_op jit(solution)/shard_map/ppermute | solution.py:409
  97.8 6.4 %copy-start.3 = (bf16[16,2304]{1,0:T(8,128)(2,1)}, bf16[16,2304]{1,0:T(8,128)(2,1)S(1)}, u32[]{:S(2)}) copy-start(bf16[16,2304]{1,0:T(8,128)(2,1)S(1)} %collective-permute-done.5.refs_2_) | copy-start | bytes 221188
  97.8 6.4 %collective-permute-start.10 = (bf16[16,2304]{1,0:T(8,128)(2,1)}, bf16[16,2304]{1,0:T(8,128)(2,1)S(1)}, u32[]{:S(2)}, u32[]{:S(2)}) collective-permute-start(bf16[16,2304]{1,0:T(8,128)(2,1)} %get-tuple-element.21), channel_id=1, source_target_pairs={{0,7},{1,0},{2,1},{3,2},{4,3},{5,4},{6,5},{7,6},{8,15},{9,8},{10,9... | collective-permute-start | bytes 221192 | tf_op jit(solution)/shard_map/ppermute | solution.py:409
  99.9 4.3 %copy-start.4 = (bf16[16,2304]{1,0:T(8,128)(2,1)}, bf16[16,2304]{1,0:T(8,128)(2,1)S(1)}, u32[]{:S(2)}) copy-start(bf16[16,2304]{1,0:T(8,128)(2,1)S(1)} %collective-permute-done.6.refs_3_) | copy-start | bytes 221188
  100.0 4.3 %copy-start.5 = (bf16[16,2304]{1,0:T(8,128)(2,1)}, bf16[16,2304]{1,0:T(8,128)(2,1)S(1)}, u32[]{:S(2)}) copy-start(bf16[16,2304]{1,0:T(8,128)(2,1)S(1)} %collective-permute-done.7.refs_4_) | copy-start | bytes 221188
  100.0 4.3 %copy-start.6 = (bf16[16,2304]{1,0:T(8,128)(2,1)}, bf16[16,2304]{1,0:T(8,128)(2,1)S(1)}, u32[]{:S(2)}) copy-start(bf16[16,2304]{1,0:T(8,128)(2,1)S(1)} %collective-permute-done.8.refs_5_) | copy-start | bytes 221188
  101.5 2.7 %copy-start.7 = (bf16[16,2304]{1,0:T(8,128)(2,1)}, bf16[16,2304]{1,0:T(8,128)(2,1)S(1)}, u32[]{:S(2)}) copy-start(bf16[16,2304]{1,0:T(8,128)(2,1)S(1)} %collective-permute-done.9.refs_6_) | copy-start | bytes 221188
  104.2 0.6 copy-start.8
